TPU v7x, 128 devices: a whole 4x4x4 slice. The times are simulated.
128 devices in a mesh: member: 4 (over y_lo, core), band: 32 (over y_hi, x, z).
Axes of the slice: x: 4, y: 4 (y_hi: 2, y_lo: 2; y = y_hi * 2 + y_lo), z: 4, core: 2. Of those that a mesh axis runs over, the one named last changes fastest.
Arguments:
- starting_condition: bfloat16 [16, 256, 64, 1440], P('member', 'band'), may hold values from -6 to 6
- filter_kernel_tensor: bfloat16 [3, 3, 64, 64], replicated, may hold values from -0.25 to 0.25
- filter_offset_vector: float32 [64], replicated, may hold values from -3 to 3
- measured_cell_position: int32 [65536], P('band'), may hold values from 0 to 737279
- measured_slot_number: int32 [32], P('band'), may hold values from 512 to 2048, as said below
- measured_reading: float32 [65536], P('band'), may hold values from -6 to 6
- measured_precision_factor: float32 [65536], P('band'), may hold values from 0.002 to 0.02
Outputs:
- analysis: bfloat16 [16, 256, 64, 1440], P('member', 'band')
Inputs may be any that keep to these rules, and one draw needn't show every extreme that they name: `measured_slot_number`: some band has all 2048 slots live.
All inputs are finite; a program needn't handle non-finite values.
Results may differ from a plain program's by a relative error of at most 0.0071.
Values may be sent and summed in bfloat16 or wider, within the bound.
A program may use at most 192 MiB of HBM per device.

v0:
```python
import jax
import jax.numpy as jnp
from jax import lax
from jax.sharding import PartitionSpec as P

STEPS = 2
NS_STEPS = 16


def extended(block, sides, width):
    for axis, dim in sides:
        count = lax.axis_size(axis)
        forward = [(i, i + 1) for i in range(count - 1)]
        backward = [(target, source) for source, target in forward]
        low = lax.ppermute(
            lax.slice_in_dim(block, block.shape[dim] - width, None, axis=dim), axis, forward
        )
        high = lax.ppermute(lax.slice_in_dim(block, 0, width, axis=dim), axis, backward)
        block = jnp.concatenate([low, block, high], axis=dim)
    return block


def kernel_mats(filter_kernel_tensor):
    width = filter_kernel_tensor.shape[2]
    return [
        jnp.transpose(filter_kernel_tensor[offset], (1, 0, 2)).reshape(width, 3 * width)
        for offset in range(3)
    ]


def advance(padded, matrices, filter_offset_vector):
    height = padded.shape[1] - 2
    stacked = jnp.concatenate(
        [jnp.roll(padded, 1, axis=3), padded, jnp.roll(padded, -1, axis=3)], axis=2
    )
    total = jnp.einsum(
        "oc,mrcl->mrol", matrices[0], stacked[:, 0:height], preferred_element_type=jnp.float32
    )
    total = total + jnp.einsum(
        "oc,mrcl->mrol", matrices[1], stacked[:, 1 : height + 1], preferred_element_type=jnp.float32
    )
    total = total + jnp.einsum(
        "oc,mrcl->mrol", matrices[2], stacked[:, 2 : height + 2], preferred_element_type=jnp.float32
    )
    center = padded[:, 1 : height + 1].astype(jnp.float32)
    return (center + jnp.tanh(total + filter_offset_vector[None, None, :, None])).astype(
        jnp.bfloat16
    )


def transform(gram, drive, ensemble_vectors):
    highest = lax.Precision.HIGHEST
    eye = jnp.eye(ensemble_vectors, dtype=jnp.float32)
    system = eye + gram / (ensemble_vectors - 1.0)
    scale = jnp.trace(system)
    iterate = system / scale
    root = eye
    for number in range(NS_STEPS):
        factor = 0.5 * (3.0 * eye - jnp.dot(root, iterate, precision=highest))
        iterate = jnp.dot(iterate, factor, precision=highest)
        root = jnp.dot(factor, root, precision=highest)
    spread = root / jnp.sqrt(scale)
    inverse = jnp.dot(root, root, precision=highest)
    mean_weights = jnp.dot(inverse, drive, precision=highest) / (scale * (ensemble_vectors - 1.0))
    centering = eye - 1.0 / ensemble_vectors
    mixing = 1.0 / ensemble_vectors + jnp.dot(
        centering, mean_weights[:, None] + spread, precision=highest
    )
    return mixing.astype(jnp.bfloat16)


def local(
    starting_condition,
    filter_kernel_tensor,
    filter_offset_vector,
    measured_cell_position,
    measured_slot_number,
    measured_reading,
    measured_precision_factor,
):
    matrices = kernel_mats(filter_kernel_tensor)
    strip_resident_runs = starting_condition.shape[0]
    model_grids = starting_condition
    for number in range(STEPS):
        padded = extended(model_grids, (("band", 1),), 1)
        model_grids = advance(padded, matrices, filter_offset_vector)
    flat_fields = model_grids.reshape(strip_resident_runs, -1)
    predicted_local = jnp.take(flat_fields, measured_cell_position, axis=1).astype(jnp.float32)
    predicted = lax.all_gather(
        predicted_local.astype(jnp.bfloat16), "member", axis=0, tiled=True
    ).astype(predicted_local.dtype)
    ensemble_vectors = predicted.shape[0]
    slots = jnp.arange(measured_cell_position.shape[0], dtype=jnp.int32)
    live = (slots < measured_slot_number[0]).astype(jnp.float32)
    mean = jnp.mean(predicted, axis=0)
    anomaly = predicted - mean[None, :]
    weighted = anomaly * (measured_precision_factor * live)[None, :]
    gram_part = jnp.dot(weighted, anomaly.T, precision=lax.Precision.HIGHEST)
    drive_part = jnp.dot(weighted, measured_reading - mean, precision=lax.Precision.HIGHEST)
    gram, drive = lax.psum((gram_part, drive_part), "band")
    mixing = transform(gram, drive, ensemble_vectors)
    column_start = lax.axis_index("member") * strip_resident_runs
    owned = lax.dynamic_slice_in_dim(mixing, column_start, strip_resident_runs, 1)
    initial = jnp.zeros(model_grids.shape, jnp.float32)
    piece = lax.all_gather(model_grids, "member", axis=0, tiled=True)
    share = lax.slice_in_dim(owned, 0, piece.shape[0], axis=0)
    return (
        initial + jnp.einsum("jrcl,jk->krcl", piece, share, preferred_element_type=jnp.float32)
    ).astype(jnp.bfloat16)


def solution(mesh):
    return jax.shard_map(
        local,
        mesh=mesh,
        in_specs=(
            P("member", "band", None, None),
            P(),
            P(),
            P("band"),
            P("band"),
            P("band"),
            P("band"),
        ),
        out_specs=P("member", "band", None, None),
        check_vma=False,
    )
```

profile of v0, /device:TPU:7, one launch (start us, length us, event | category | flops | bytes accessed | tf_op | source)
XLA Modules:
  0.0 509.1 jit_solution(4374819341090139670)
XLA Ops:
  8.1 3.5 collective-permute-start
  11.6 4.3 collective-permute-start.1
  17.1 14.1 %collective-permute-done = bf16[4,1,64,1440]{3,2,1,0:T(8,128)(2,1)S(1)} collective-permute-done((bf16[4,1,64,1440]{3,2,1,0:T(8,128)(2,1)S(1)}, bf16[4,1,64,1440]{3,2,1,0:T(8,128)(2,1)S(1)}, u32[]{:S(2)}, u32[]{:S(2)}) %collective-permute-start) | collective-permute-done | bytes 737312 | tf_op jit(solution)/shard_map/ppermute | solution.py:15
  31.3 3.5 constant_dynamic-update-slice_fusion.1
  34.9 7.8 %fusion.63 = (bf16[4,10,64,1439]{3,2,1,0:T(8,128)(2,1)}, bf16[4,10,64,1439]{3,2,1,0:T(8,128)(2,1)}) fusion(bf16[4,10,64,1440]{3,2,1,0:T(8,128)(2,1)S(1)} %constant_dynamic-update-slice_fusion), kind=kLoop, calls=%fused_computation.105 | loop fusion | bytes 29470720 | tf_op jit(solution)/shard_map/jit(_roll_static)/slice | solution.py:34
  43.0 23.6 %fusion.4 = bf16[4,10,192,1440]{3,2,1,0:T(8,128)(2,1)} fusion(bf16[4,10,64,1]{3,2,1,0:T(8,128)(2,1)S(1)} %get-tuple-element.10, bf16[4,10,64,1439]{3,2,1,0:T(8,128)(2,1)} %get-tuple-element.12, bf16[4,10,64,1439]{3,2,1,0:T(8,128)(2,1)} %get-tuple-element.11, bf16[4,10,64,1]{3,2,1,0:T(8,128)(2,1)S(1)} %get-tuple-element.9, bf16[4,10,64,1440]{3,2,1,0:T(8,128)(2,1)} %copy-done), kind=kLoop, calls=%fused_computation.12 | loop fusion | flops 110592000 | bytes 44236800 | tf_op jit(solution)/shard_map/concatenate | solution.py:33
  66.6 14.8 %fusion.96 = f32[4,8,1440,64]{2,3,1,0:T(8,128)} fusion(bf16[4,10,192,1440]{3,2,1,0:T(8,128)(2,1)} %fusion.4, bf16[64,192,1,1]{0,1,3,2:T(8,128)(2,1)S(1)} %bitcast.161), kind=kOutput, calls=%fused_computation.138 | convolution fusion | flops 1132462080 | bytes 33939456 | tf_op jit(solution)/shard_map/oc,mrcl->mrol/dot_general | solution.py:36
  81.4 14.8 %fusion.97 = f32[4,8,1440,64]{2,3,1,0:T(8,128)} fusion(bf16[4,10,192,1440]{3,2,1,0:T(8,128)(2,1)} %fusion.4, bf16[64,192,1,1]{0,1,3,2:T(8,128)(2,1)S(1)} %bitcast.165), kind=kOutput, calls=%fused_computation.139 | convolution fusion | flops 1132462080 | bytes 33939456 | tf_op jit(solution)/shard_map/oc,mrcl->mrol/dot_general | solution.py:39
  96.3 18.0 %fusion.7 = bf16[4,8,64,1440]{3,2,1,0:T(8,128)(2,1)S(1)} fusion(f32[4,8,1440,64]{2,3,1,0:T(8,128)} %fusion.96, f32[4,8,1440,64]{2,3,1,0:T(8,128)} %fusion.97, bf16[4,8,64,1440]{3,2,1,0:T(8,128)(2,1)} %param.7, bf16[4,10,192,1440]{3,2,1,0:T(8,128)(2,1)} %fusion.4, bf16[64,192,1,1]{0,1,3,2:T(8,128)(2,1)S(1)} %bitcast.163, f32[64]{0:T(128)S(1)} %copy-done.1), kind=kOutput, calls=%fused_computation.18 | convolution fusion | flops 1150156800 | bytes 57532672 | tf_op jit(solution)/shard_map/oc,mrcl->mrol/dot_general | solution.py:42
  116.3 5.8 %collective-permute-start.3 = (bf16[4,1,64,1440]{3,2,1,0:T(8,128)(2,1)S(1)}, bf16[4,1,64,1440]{3,2,1,0:T(8,128)(2,1)S(1)}, u32[]{:S(2)}, u32[]{:S(2)}) collective-permute-start(bf16[4,1,64,1440]{3,2,1,0:T(8,128)(2,1)S(1)} %get-tuple-element.14), channel_id=1, source_target_pairs={{1,0},{2,1},{3,2},{4,3},{5,4},{6,5},{7,6},{8,7},{9,8},{10,9},{11,1... | collective-permute-start | bytes 2211848 | tf_op jit(solution)/shard_map/ppermute | solution.py:18
  122.2 14.1 %collective-permute-done.2 = bf16[4,1,64,1440]{3,2,1,0:T(8,128)(2,1)S(1)} collective-permute-done((bf16[4,1,64,1440]{3,2,1,0:T(8,128)(2,1)S(1)}, bf16[4,1,64,1440]{3,2,1,0:T(8,128)(2,1)S(1)}, u32[]{:S(2)}, u32[]{:S(2)}) %collective-permute-start.2) | collective-permute-done | bytes 737312 | tf_op jit(solution)/shard_map/ppermute | solution.py:15
  138.2 7.3 %fusion.61 = (bf16[4,10,64,1439]{3,2,1,0:T(8,128)(2,1)}, bf16[4,10,64,1439]{3,2,1,0:T(8,128)(2,1)}) fusion(bf16[4,10,64,1440]{3,2,1,0:T(8,128)(2,1)S(1)} %pad_maximum_fusion.8), kind=kLoop, calls=%fused_computation.103 | loop fusion | bytes 29470720 | tf_op jit(solution)/shard_map/jit(_roll_static)/slice | solution.py:34
  145.5 37.6 %fusion.2 = bf16[4,10,192,1440]{3,2,1,0:T(8,128)(2,1)} fusion(bf16[4,10,64,1439]{3,2,1,0:T(8,128)(2,1)} %get-tuple-element.8, bf16[4,1,64,1440]{3,2,1,0:T(8,128)(2,1)S(1)} %collective-permute-done.3, bf16[4,8,64,1440]{3,2,1,0:T(8,128)(2,1)S(1)} %fusion.7, bf16[4,1,64,1440]{3,2,1,0:T(8,128)(2,1)S(1)} %collective-permute-done.2, ...), kind=kLoop, calls=%fused_computation.4 | loop fusion | flops 243302400 | bytes 44226560 | tf_op jit(solution)/shard_map/concatenate | solution.py:33
  183.1 14.8 %fusion.99 = f32[4,8,1440,64]{2,3,1,0:T(8,128)} fusion(bf16[4,10,192,1440]{3,2,1,0:T(8,128)(2,1)} %fusion.2, bf16[64,192,1,1]{0,1,3,2:T(8,128)(2,1)S(1)} %bitcast.166), kind=kOutput, calls=%fused_computation.141 | convolution fusion | flops 1132462080 | bytes 33939456 | tf_op jit(solution)/shard_map/oc,mrcl->mrol/dot_general | solution.py:39
  197.9 14.8 %fusion.98 = f32[4,8,1440,64]{2,3,1,0:T(8,128)} fusion(bf16[4,10,192,1440]{3,2,1,0:T(8,128)(2,1)} %fusion.2, bf16[64,192,1,1]{0,1,3,2:T(8,128)(2,1)S(1)} %bitcast.162), kind=kOutput, calls=%fused_computation.140 | convolution fusion | flops 1132462080 | bytes 33939456 | tf_op jit(solution)/shard_map/oc,mrcl->mrol/dot_general | solution.py:36
  212.7 19.1 %fusion.6 = bf16[4,8,64,1440]{3,2,1,0:T(8,128)(2,1)} fusion(f32[4,8,1440,64]{2,3,1,0:T(8,128)} %fusion.98, f32[4,8,1440,64]{2,3,1,0:T(8,128)} %fusion.99, bf16[4,8,64,1440]{3,2,1,0:T(8,128)(2,1)S(1)} %fusion.7, bf16[4,10,192,1440]{3,2,1,0:T(8,128)(2,1)} %fusion.2, bf16[64,192,1,1]{0,1,3,2:T(8,128)(2,1)S(1)} %bitcast.164, f32[64]{0:T(128)S(1)} %copy-done.1), kind=kOutput, calls=%fused_computation.16 | convolution fusion | flops 1150156800 | bytes 57532672 | tf_op jit(solution)/shard_map/oc,mrcl->mrol/dot_general | solution.py:42
  232.5 13.8 %reshape.50 = bf16[2949120]{0:T(1024)(128)(2,1)} reshape(bf16[4,8,64,1440]{3,2,1,0:T(8,128)(2,1)} %fusion.6) | data formatting | bytes 11796480
  246.4 8.4 %reshape.26 = bf16[4,737280]{1,0:T(4,128)(2,1)} reshape(bf16[2949120]{0:T(1024)(128)(2,1)} %reshape.50) | data formatting | bytes 11796480 | tf_op jit(solution)/shard_map/reshape | solution.py:87
  254.8 25.2 %gather_fusion = bf16[2048,4]{0,1:T(4,128)(2,1)S(1)} fusion(bf16[4,737280]{1,0:T(4,128)(2,1)} %reshape.26, s32[2048]{0:T(1024)S(1)} %fusion.43), kind=kCustom, calls=%fused_computation | custom fusion | bytes 40960 | tf_op jit(solution)/shard_map/jit(_take)/gather | solution.py:88
  280.0 8.0 %all-gather = bf16[4,4,2048]{2,1,0:T(4,128)(2,1)S(1)} all-gather(bf16[1,4,2048]{2,1,0:T(4,128)(2,1)S(1)} %select_bitcast_fusion), channel_id=1, replica_groups=mesh['member'=4,'band'=32] {'member'}, dimensions={0}, use_global_device_ids=true | all-gather | bytes 81920 | tf_op jit(solution)/shard_map/all_gather | solution.py:89
  288.6 80.6 %all-reduce = (f32[16,16]{1,0:T(8,128)S(1)}, f32[16]{0:T(128)S(1)}) all-reduce(f32[16,16]{1,0:T(8,128)S(1)} %fusion.29, f32[16]{0:T(128)S(1)} %convolution_bitcast_fusion.1), channel_id=1, replica_groups=mesh['member'=4,'band'=32] {'band'}, use_global_device_ids=true, to_apply=%region_1.2 | all-reduce | flops 272 | bytes 2176 | tf_op jit(solution)/shard_map/psum | solution.py:100
  379.7 88.9 %all-gather.3.cloned.1.call-done = bf16[16,8,64,1440]{3,2,1,0:T(8,128)(2,1)} async-done(((bf16[4,8,64,1440]{3,2,1,0:T(8,128)(2,1)}), bf16[16,8,64,1440]{3,2,1,0:T(8,128)(2,1)}) %all-gather.3.cloned.1.call-update) | async-done | bytes 23592976 | tf_op jit(solution)/shard_map/all_gather | solution.py:105
  468.7 26.4 %fusion.8 = bf16[4,8,64,1440]{3,0,2,1:T(4,128)(2,1)} fusion(bf16[16,8,64,1440]{3,2,1,0:T(8,128)(2,1)} %all-gather.3.cloned.1.call-done, f32[16,16]{0,1:T(8,128)S(1)} %fusion.37, s32[]{:T(128)S(6)} %select_n.20), kind=kOutput, calls=%fused_computation.19 | convolution fusion | flops 97321088 | bytes 29493252 | tf_op jit(solution)/shard_map/jrcl,jk->krcl/dot_general | solution.py:108
  495.1 6.9 %copy.34 = bf16[4,8,64,1440]{3,2,1,0:T(8,128)(2,1)} copy(bf16[4,8,64,1440]{3,0,2,1:T(4,128)(2,1)} %fusion.8) | data formatting | bytes 11796480 | tf_op jit(solution)/shard_map/convert_element_type | solution.py:109
  (85 shorter events, 16.9 us)
Async XLA Ops:
  6.5 462.1 %all-gather.3.cloned.1.call-start = ((), (), s32[]{:S(2)}) async-start(), calls=%async_computation | async-start | bytes 31457280 | tf_op jit(solution)/shard_map/all_gather | solution.py:105
  8.1 23.2 %collective-permute-start = (bf16[4,1,64,1440]{3,2,1,0:T(8,128)(2,1)S(1)}, bf16[4,1,64,1440]{3,2,1,0:T(8,128)(2,1)S(1)}, u32[]{:S(2)}, u32[]{:S(2)}) collective-permute-start(bf16[4,1,64,1440]{3,2,1,0:T(8,128)(2,1)S(1)} %get-tuple-element.16), channel_id=1, source_target_pairs={{0,1},{1,2},{2,3},{3,4},{4,5},{5,6},{6,7},{7,8},{8,9},{9,10},{10,1... | collective-permute-start | bytes 2211848 | tf_op jit(solution)/shard_map/ppermute | solution.py:15
  11.6 23.2 %collective-permute-start.1 = (bf16[4,1,64,1440]{3,2,1,0:T(8,128)(2,1)S(1)}, bf16[4,1,64,1440]{3,2,1,0:T(8,128)(2,1)S(1)}, u32[]{:S(2)}, u32[]{:S(2)}) collective-permute-start(bf16[4,1,64,1440]{3,2,1,0:T(8,128)(2,1)S(1)} %get-tuple-element.15), channel_id=1, source_target_pairs={{1,0},{2,1},{3,2},{4,3},{5,4},{6,5},{7,6},{8,7},{9,8},{10,9},{11,1... | collective-permute-start | bytes 2211848 | tf_op jit(solution)/shard_map/ppermute | solution.py:18
  34.8 7.8 %copy-start = (bf16[4,10,64,1440]{3,2,1,0:T(8,128)(2,1)}, bf16[4,10,64,1440]{3,2,1,0:T(8,128)(2,1)S(1)}, u32[]{:S(2)}) copy-start(bf16[4,10,64,1440]{3,2,1,0:T(8,128)(2,1)S(1)} %constant_dynamic-update-slice_fusion) | copy-start | bytes 22118404
  81.4 14.8 %copy-start.1 = (f32[64]{0:T(128)S(1)}, f32[64]{0:T(128)}, u32[]{:S(2)}) copy-start(f32[64]{0:T(128)} %param.9) | copy-start | bytes 772
  114.4 21.9 %collective-permute-start.2 = (bf16[4,1,64,1440]{3,2,1,0:T(8,128)(2,1)S(1)}, bf16[4,1,64,1440]{3,2,1,0:T(8,128)(2,1)S(1)}, u32[]{:S(2)}, u32[]{:S(2)}) collective-permute-start(bf16[4,1,64,1440]{3,2,1,0:T(8,128)(2,1)S(1)} %get-tuple-element.13), channel_id=1, source_target_pairs={{0,1},{1,2},{2,3},{3,4},{4,5},{5,6},{6,7},{7,8},{8,9},{9,10},{10,1... | collective-permute-start | bytes 2211848 | tf_op jit(solution)/shard_map/ppermute | solution.py:15
  116.3 20.8 %collective-permute-start.3 = (bf16[4,1,64,1440]{3,2,1,0:T(8,128)(2,1)S(1)}, bf16[4,1,64,1440]{3,2,1,0:T(8,128)(2,1)S(1)}, u32[]{:S(2)}, u32[]{:S(2)}) collective-permute-start(bf16[4,1,64,1440]{3,2,1,0:T(8,128)(2,1)S(1)} %get-tuple-element.14), channel_id=1, source_target_pairs={{1,0},{2,1},{3,2},{4,3},{5,4},{6,5},{7,6},{8,7},{9,8},{10,9},{11,1... | collective-permute-start | bytes 2211848 | tf_op jit(solution)/shard_map/ppermute | solution.py:18
  212.7 19.8 %copy-start.2 = (s32[2048]{0:T(1024)S(1)}, s32[2048]{0:T(1024)}, u32[]{:S(2)}) copy-start(s32[2048]{0:T(1024)} %param.10) | copy-start | bytes 24580
  212.7 19.8 %copy-start.3 = (f32[2048]{0:T(1024)S(1)}, f32[2048]{0:T(1024)}, u32[]{:S(2)}) copy-start(f32[2048]{0:T(1024)} %param.13) | copy-start | bytes 24580
  232.5 55.5 %copy-start.4 = (f32[2048]{0:T(1024)S(1)}, f32[2048]{0:T(1024)}, u32[]{:S(2)}) copy-start(f32[2048]{0:T(1024)} %param.12) | copy-start | bytes 24580
Sparse Core Ops, SparseCore 0:
  231.9 236.6 all-gather.2
where the time goes:
time: 519 us; the launch traced here: 509 us
  matrix products  132 us (25%)
  waiting for transfers between devices  118 us (23%)
  blocking collectives  88.6 us (17%)
  local copies, waits for them, and re-layouts  76.1 us (15%)
  other arithmetic  63 us (12%)
  between operations  15.9 us (3%)
  starting transfers between devices  15.6 us (3%)
    all_gather x1, waiting for transfers between devices, local(): piece = lax.all_gather(model_grids, 'member', axis=0, tiled=True)  88.9 us
    psum x1, blocking collectives, local(): gram, drive = lax.psum((gram_part, drive_part), 'band')  80.6 us
    concatenate x2, other arithmetic, advance(): jnp.concatenate([jnp.roll(padded, 1, axis=3), padded, jnp.roll(padded, -1...  61.2 us
    dot_general x2, matrix products, advance(): jnp.einsum('oc,mrcl->mrol', matrices[2], stacked[:, 2:height + 2], prefer...  37.1 us
    dot_general x2, matrix products, advance(): jnp.einsum('oc,mrcl->mrol', matrices[1], stacked[:, 1:height + 1], prefer...  29.7 us
    dot_general x2, matrix products, advance(): jnp.einsum('oc,mrcl->mrol', matrices[0], stacked[:, 0:height], preferred_...  29.5 us
    ppermute x2, waiting for transfers between devices, extended(): lax.ppermute(lax.slice_in_dim(block, block.shape[dim] - width, None, axis...  28.2 us
    dot_general x1, matrix products, local(): jnp.einsum('jrcl,jk->krcl', piece, share, preferred_element_type=jnp.floa...  26.4 us
  transfers between devices with their start and end apart: 5, of which 4 were waited for; matrix products, arithmetic and copies ran while one was open for 12% of the time, Pallas kernels for 0%

commit v1 on v0

v1 whole, which is shorter than its diff:
```python
import functools

import jax
import jax.numpy as jnp
from jax import lax
from jax.experimental import pallas as pl
from jax.experimental.pallas import tpu as pltpu
from jax.sharding import PartitionSpec as P

NS_STEPS = 16
LON = 1440
WIDE = 1536
MAIN = 1408
PACK = 5760
F32 = jnp.float32
BF16 = jnp.bfloat16
ANY = pl.BlockSpec(memory_space=pl.ANY)
VM = pl.BlockSpec(memory_space=pltpu.VMEM)
SM = pl.BlockSpec(memory_space=pltpu.SMEM)


def remote(src, dst, send, recv, peer):
    return pltpu.make_async_remote_copy(
        src_ref=src, dst_ref=dst, send_sem=send, recv_sem=recv, device_id=peer
    )


def widen(x):
    last = jnp.concatenate(
        [x[:, MAIN:LON], x[:, 0:32], x[:, 0:32], x[:, MAIN:LON]], axis=1
    )
    return jnp.concatenate([x[:, :MAIN], last], axis=1)


def conv_rows(src, count, weights, bias, acc_near, acc_far, emit):
    def body(q, carry):
        row = src[q]
        taps = jnp.concatenate(
            [pltpu.roll(row, 1, 1), row, pltpu.roll(row, WIDE - 1, 1)], axis=0
        )
        part = jnp.dot(weights, taps, preferred_element_type=F32)
        total = acc_near[...] + part[128:192]
        acc_near[...] = acc_far[...] + part[64:128]
        acc_far[...] = part[0:64]

        @pl.when(q >= 2)
        def _():
            center = src[q - 1].astype(F32)
            emit(q - 2, (center + jnp.tanh(total + bias)).astype(BF16))

        return carry

    lax.fori_loop(0, count, body, 0)


def forecast_kernel(
    x_ref, w_ref, b_ref, f_ref,
    xin, wide, mid, acc_near, acc_far, rem, fields,
    load_sem, halo_send, halo_recv, start_send, start_recv,
    keep_sem, y_send, y_recv, c_send, c_recv, g_send, g_recv,
):
    g = lax.axis_index("member")
    b = lax.axis_index("band")
    ypeer = {"member": g ^ 2}
    cpeer = {"member": g ^ 1}
    up = {"band": lax.rem(b + 1, 32)}
    down = {"band": lax.rem(b + 31, 32)}
    barrier = pltpu.get_barrier_semaphore()
    for peer in (ypeer, cpeer, up, down):
        pl.semaphore_signal(barrier, inc=1, device_id=peer)

    def load(m):
        return pltpu.make_async_copy(x_ref.at[m], xin.at[m, 2:10], load_sem.at[m])

    for m in (1, 2, 3, 0):
        load(m).start()
    pl.semaphore_wait(barrier, 4)

    def halo_up(slot, src):
        return remote(src, xin.at[slot, 0:2], halo_send.at[slot, 0], halo_recv.at[slot, 0], up)

    def halo_down(slot, src):
        return remote(src, xin.at[slot, 10:12], halo_send.at[slot, 1], halo_recv.at[slot, 1], down)

    def halo_start(slot, high, low):
        @pl.when(b < 31)
        def _():
            halo_up(slot, high).start()

        @pl.when(b > 0)
        def _():
            halo_down(slot, low).start()

    def own_halo(m):
        halo_start(m, x_ref.at[m, 6:8], x_ref.at[m, 0:2])

    def start_copy():
        return remote(x_ref.at[0], xin.at[4, 2:10], start_send, start_recv, ypeer)

    own_halo(1)
    start_copy().start()
    for m in (2, 3, 0):
        own_halo(m)

    weights = w_ref[...]
    bias = b_ref[...]

    def keep(slot, d, m):
        return pltpu.make_async_copy(fields.at[slot], f_ref.at[d, m], keep_sem.at[slot])

    def y_copy(m):
        return remote(f_ref.at[0, m], f_ref.at[2, m], y_send.at[m], y_recv.at[m], ypeer)

    def c_copy(m):
        return remote(f_ref.at[0, m], f_ref.at[1, m], c_send.at[m], c_recv.at[m], cpeer)

    def g_copy(m):
        return remote(f_ref.at[2, m], f_ref.at[3, m], g_send.at[m], g_recv.at[m], cpeer)

    def iteration(i, carry):
        slot = jnp.where(i == 4, 4, lax.rem(i + 1, 4))

        @pl.when(i < 4)
        def _():
            load(slot).wait()

        @pl.when(b > 0)
        def _():
            halo_up(slot, x_ref.at[0, 6:8]).wait_recv()

        @pl.when(b < 31)
        def _():
            halo_down(slot, x_ref.at[0, 0:2]).wait_recv()

        @pl.when(b == 0)
        def _():
            xin[slot, 0:2] = jnp.zeros((2, 64, LON), BF16)

        @pl.when(b == 31)
        def _():
            xin[slot, 10:12] = jnp.zeros((2, 64, LON), BF16)

        def spread(r, c):
            wide[r] = widen(xin[slot, r])
            return c

        lax.fori_loop(0, 12, spread, 0)

        def emit_mid(r, value):
            mid[r] = value

        conv_rows(wide, 12, weights, bias, acc_near, acc_far, emit_mid)

        @pl.when(b == 0)
        def _():
            mid[0] = jnp.zeros((64, WIDE), BF16)

        @pl.when(b == 31)
        def _():
            mid[9] = jnp.zeros((64, WIDE), BF16)

        def emit_field(r, value):
            half = r // 4
            offset = pl.multiple_of(lax.rem(r, 4) * MAIN, 128)
            fields[slot, half, :, pl.ds(offset, MAIN)] = value[:, :MAIN]
            rem[r] = value[:, MAIN:WIDE]

        conv_rows(mid, 10, weights, bias, acc_near, acc_far, emit_field)
        lane = lax.broadcasted_iota(jnp.int32, (64, 128), 1)
        for half in range(2):
            tail = rem[4 * half]
            for j in range(1, 4):
                tail = jnp.where(lane < 32 * j, tail, pltpu.roll(rem[4 * half + j], 32 * j, 1))
            fields[slot, half, :, 4 * MAIN : PACK] = tail

        @pl.when(i < 4)
        def _():
            keep(slot, 0, slot).start()
            keep(slot, 0, slot).wait()
            c_copy(slot).start()

        @pl.when(i < 3)
        def _():
            y_copy(slot).start()

        @pl.when(i == 2)
        def _():
            start_copy().wait_recv()
            halo_start(4, xin.at[4, 8:10], xin.at[4, 2:4])

        @pl.when(i == 4)
        def _():
            keep(4, 2, 0).start()
            keep(4, 2, 0).wait()
            g_copy(0).start()

        return carry

    lax.fori_loop(0, 5, iteration, 0)

    start_copy().wait_send()
    for slot in range(5):
        @pl.when(b < 31)
        def _():
            halo_up(slot, x_ref.at[0, 6:8]).wait_send()

        @pl.when(b > 0)
        def _():
            halo_down(slot, x_ref.at[0, 0:2]).wait_send()

    for m in (1, 2, 3):
        y_copy(m).wait_recv()
        g_copy(m).start()
    for m in (1, 2, 3):
        y_copy(m).wait_send()
    for m in range(4):
        c_copy(m).wait()
        g_copy(m).wait()


def run_forecast(x, weights, bias):
    dma = pltpu.SemaphoreType.DMA
    return pl.pallas_call(
        forecast_kernel,
        out_shape=jax.ShapeDtypeStruct((4, 4, 2, 64, PACK), BF16),
        in_specs=[ANY, VM, VM],
        out_specs=ANY,
        scratch_shapes=[
            pltpu.VMEM((5, 12, 64, LON), BF16),
            pltpu.VMEM((12, 64, WIDE), BF16),
            pltpu.VMEM((10, 64, WIDE), BF16),
            pltpu.VMEM((64, WIDE), F32),
            pltpu.VMEM((64, WIDE), F32),
            pltpu.VMEM((8, 64, 128), BF16),
            pltpu.VMEM((5, 2, 64, PACK), BF16),
            dma((4,)), dma((5, 2)), dma((5, 2)), dma, dma,
            dma((5,)), dma((4,)), dma((4,)), dma((4,)), dma((4,)), dma((4,)), dma((4,)),
        ],
        compiler_params=pltpu.CompilerParams(
            collective_id=1, has_side_effects=True, vmem_limit_bytes=56 << 20
        ),
        name="forecast",
    )(x, weights, bias)


def pick_kernel(index_ref, lane_ref, f_ref, p_ref, fv, wide, slab, sem):
    copy = pltpu.make_async_copy(f_ref.at[0], fv, sem)
    copy.start()
    copy.wait()
    for m in range(4):
        for half in range(2):
            widen_field(fv.at[m, half], wide.at[m], half)
    pick_loop(index_ref, lane_ref, p_ref, wide, slab)


def widen_field(src, dst, half):
    for block in range(45):
        start = block * 128
        dst[start + half * 64 : start + half * 64 + 64, :] = src[:, start : start + 128].astype(F32)


def pick_loop(index_ref, lane_ref, p_ref, wide, slab):
    def group(n, carry):
        base = n * 128

        def fetch(t, c):
            for u in range(8):
                slot = t * 8 + u
                code = index_ref[base + slot]
                for m in range(4):
                    slab[m, pl.ds(slot, 1), :] = wide[m, pl.ds(code, 1), :]
            return c

        lax.fori_loop(0, 16, fetch, 0)
        lanes = lane_ref[pl.ds(pl.multiple_of(base, 128), 128), :]
        hot = lax.broadcasted_iota(jnp.int32, (128, 128), 1) == lanes
        total = jnp.zeros((8, 128), F32)
        rows = lax.broadcasted_iota(jnp.int32, (8, 128), 0)
        for m in range(4):
            masked = jnp.where(hot, slab[m], 0.0).astype(BF16)
            ones = jnp.where(rows == m, 1.0, 0.0).astype(BF16)
            total = total + lax.dot_general(
                ones, masked, (((1,), (1,)), ((), ())), preferred_element_type=F32
            )
        p_ref[:, pl.ds(pl.multiple_of(base, 128), 128)] = total
        return carry

    lax.fori_loop(0, 16, group, 0)


def run_pick(index, lane, fields):
    return pl.pallas_call(
        pick_kernel,
        out_shape=jax.ShapeDtypeStruct((8, 2048), F32),
        in_specs=[SM, VM, ANY],
        out_specs=VM,
        scratch_shapes=[
            pltpu.VMEM((4, 2, 64, PACK), BF16),
            pltpu.VMEM((4, PACK, 128), F32),
            pltpu.VMEM((4, 128, 128), F32),
            pltpu.SemaphoreType.DMA,
        ],
        compiler_params=pltpu.CompilerParams(vmem_limit_bytes=56 << 20),
        name="pick",
    )(index, lane, fields)


def exact(a, b, dims=(((1,), (0,)), ((), ()))):
    return lax.dot_general(
        a, b, dims, precision=lax.Precision.HIGHEST, preferred_element_type=F32
    )


def transform(gram, drive):
    n = 16
    eye = (
        lax.broadcasted_iota(jnp.int32, (n, n), 0) == lax.broadcasted_iota(jnp.int32, (n, n), 1)
    ).astype(F32)
    system = eye + gram / (n - 1.0)
    scale = jnp.sum(jnp.sum(system * eye, axis=1, keepdims=True), axis=0, keepdims=True)
    iterate = system / scale
    root = eye
    for _ in range(NS_STEPS):
        factor = 0.5 * (3.0 * eye - exact(root, iterate))
        iterate = exact(iterate, factor)
        root = exact(factor, root)
    spread = root / jnp.sqrt(scale)
    mean_weights = exact(exact(root, root), drive) / (scale * (n - 1.0))
    centering = eye - 1.0 / n
    return 1.0 / n + exact(centering, mean_weights + spread)


def stats_kernel(
    p_ref, live_ref, reading_ref, precision_ref, k_ref,
    preds, sums, p_send, p_recv, z_send, z_recv, x_send, x_recv, h_send, h_recv,
):
    g = lax.axis_index("member")
    b = lax.axis_index("band")
    z = lax.rem(b, 4)
    xx = lax.rem(b // 4, 4)
    hi = b // 16
    members = [{"member": g ^ d} for d in (1, 2, 3)]
    zs = [{"band": b - z + lax.rem(z + d, 4)} for d in (1, 2, 3)]
    xs = [{"band": hi * 16 + lax.rem(xx + d, 4) * 4 + z} for d in (1, 2, 3)]
    far = {"band": lax.rem(b + 16, 32), "member": g ^ 2}
    barrier = pltpu.get_barrier_semaphore()
    for peer in members + zs + xs + [far]:
        pl.semaphore_signal(barrier, inc=1, device_id=peer)
    pl.semaphore_wait(barrier, 10)

    preds[g] = p_ref[...]
    copies = [
        remote(p_ref, preds.at[g], p_send.at[d], p_recv.at[d], members[d]) for d in range(3)
    ]
    for c in copies:
        c.start()
    for c in copies:
        c.wait()
    predicted = jnp.concatenate([preds[d, 0:4] for d in range(4)], axis=0)
    mean = jnp.sum(predicted, axis=0, keepdims=True) * (1.0 / 16.0)
    anomaly = predicted - mean
    weighted = anomaly * (precision_ref[...] * live_ref[...])
    gram = exact(weighted, anomaly, (((1,), (1,)), ((), ())))
    drive = jnp.sum(weighted * (reading_ref[...] - mean), axis=1, keepdims=True)
    pair = jnp.concatenate([gram, drive, jnp.zeros((16, 111), F32)], axis=1)

    def reduce(stage, place, pair, peers, sends, recvs):
        sums[stage, place] = pair
        copies = [
            remote(sums.at[stage, place], sums.at[stage, place], sends.at[d], recvs.at[d], peer)
            for d, peer in enumerate(peers)
        ]
        for c in copies:
            c.start()
        for c in copies:
            c.wait()

    reduce(0, z, pair, zs, z_send, z_recv)
    pair = (sums[0, 0] + sums[0, 1]) + (sums[0, 2] + sums[0, 3])
    reduce(1, xx, pair, xs, x_send, x_recv)
    pair = (sums[1, 0] + sums[1, 1]) + (sums[1, 2] + sums[1, 3])
    reduce(2, hi, pair, [far], h_send, h_recv)
    pair = sums[2, 0] + sums[2, 1]
    mixing = transform(pair[:, 0:16], pair[:, 16:17]).astype(BF16)
    k_ref[...] = expand(mixing, g)


def expand(mixing, g):
    def iota(shape, dim):
        return lax.broadcasted_iota(jnp.int32, shape, dim)

    own = (iota((64, 16), 1) == 4 * g + iota((64, 16), 0) // 16).astype(BF16)
    column = iota((16, 256), 1)
    source = 4 * jnp.bitwise_xor(column // 64, g) + lax.rem(column // 16, 4)
    order = (iota((16, 256), 0) == source).astype(BF16)
    picked = lax.dot_general(
        own, mixing, (((1,), (1,)), ((), ())), preferred_element_type=F32
    ).astype(BF16)
    full = jnp.dot(picked, order, preferred_element_type=F32)
    same = lax.rem(iota((64, 256), 0), 16) == lax.rem(iota((64, 256), 1), 16)
    return jnp.where(same, full, 0.0).astype(BF16)


def run_stats(predicted, live, reading, precision):
    dma = pltpu.SemaphoreType.DMA
    return pl.pallas_call(
        stats_kernel,
        out_shape=jax.ShapeDtypeStruct((64, 256), BF16),
        in_specs=[VM] * 4,
        out_specs=VM,
        scratch_shapes=[
            pltpu.VMEM((4, 8, 2048), F32),
            pltpu.VMEM((3, 4, 16, 128), F32),
            dma((3,)), dma((3,)), dma((3,)), dma((3,)), dma((3,)), dma((3,)), dma((1,)), dma((1,)),
        ],
        compiler_params=pltpu.CompilerParams(collective_id=2, has_side_effects=True),
        name="stats",
    )(predicted, live, reading, precision)


def mix_kernel(k_ref, f_ref, o_ref):
    mats = k_ref[...]

    def product(lo, width):
        block = f_ref[:, :, 0, :, lo : lo + width].reshape(256, width)
        return jnp.dot(mats, block, preferred_element_type=F32).astype(BF16).reshape(4, 16, width)

    tail = product(4 * MAIN, 128)
    for j in range(4):
        o_ref[:, j, :, 0:MAIN] = product(j * MAIN, MAIN)
        o_ref[:, j, :, MAIN:LON] = tail[:, :, 32 * j : 32 * j + 32]


def run_mix(mats, fields):
    return pl.pallas_call(
        mix_kernel,
        grid=(2, 4),
        out_shape=jax.ShapeDtypeStruct((4, 8, 64, LON), BF16),
        in_specs=[
            pl.BlockSpec((64, 256), lambda h, c: (0, 0)),
            pl.BlockSpec((4, 4, 1, 16, PACK), lambda h, c: (0, 0, h, c, 0)),
        ],
        out_specs=pl.BlockSpec((4, 4, 16, LON), lambda h, c: (0, h, c, 0)),
        compiler_params=pltpu.CompilerParams(vmem_limit_bytes=56 << 20),
        name="mix",
    )(mats, fields)


def local(x, kernel, offset, position, slots, reading, precision):
    weights = jnp.transpose(kernel, (0, 2, 1, 3)).reshape(192, 192)
    fields = run_forecast(x, weights, offset[:, None])
    flat = position // LON
    lon = position - flat * LON
    row = flat // 64
    part = row // 4
    j = row - part * 4
    lane = jnp.where(lon < MAIN, j * MAIN + lon, 4 * MAIN + 32 * j + lon - MAIN)
    index = (lane // 128) * 128 + part * 64 + flat - row * 64
    lane = lax.rem(lane, 128)
    predicted = run_pick(index, lane[:, None], fields)
    live = (lax.broadcasted_iota(jnp.int32, (1, 2048), 1) < slots[0]).astype(F32)
    mats = run_stats(predicted, live, reading[None], precision[None])
    return run_mix(mats, fields)


def solution(mesh):
    return jax.shard_map(
        local,
        mesh=mesh,
        in_specs=(
            P("member", "band", None, None), P(), P(), P("band"), P("band"), P("band"), P("band"),
        ),
        out_specs=P("member", "band", None, None),
        check_vma=False,
    )
```

time: 519 us -> 244 us (0.47)
  the two profiles are of different devices: /device:TPU:7 before, /device:TPU:1 now
where the time goes in v1:
time: 244 us; the launch traced here: 243 us
  Pallas kernels  235 us (96%)
  local copies, waits for them, and re-layouts  4.54 us (2%)
  other arithmetic  2.66 us (1%)
    pallas_call x1, Pallas kernels, run_forecast(): pl.pallas_call(forecast_kernel, out_shape=jax.ShapeDtypeStruct((4, 4, 2,...  145 us
    pallas_call x1, Pallas kernels, run_stats(): pl.pallas_call(stats_kernel, out_shape=jax.ShapeDtypeStruct((64, 256), BF...  61.5 us
    pallas_call x1, Pallas kernels, run_pick(): pl.pallas_call(pick_kernel, out_shape=jax.ShapeDtypeStruct((8, 2048), F32...  15 us
    pallas_call x1, Pallas kernels, run_mix(): pl.pallas_call(mix_kernel, grid=(2, 4), out_shape=jax.ShapeDtypeStruct((4...  13.4 us

profile of v1, /device:TPU:1, one launch (start us, length us, event | category | flops | bytes accessed | tf_op | source)
XLA Modules:
  0.0 242.6 jit_solution(14140224635033180087)
XLA Ops:
  0.7 0.6 compare_convert_fusion.live_ref
  1.3 0.7 negate_select_fusion.1
  2.0 1.3 fusion.5.index_ref
  3.3 1.3 copy.11.b_ref
  4.7 1.0 copy.10
  5.7 0.8 reshape.15.w_ref
  6.5 1.3 copy.12.lane_ref
  7.9 144.7 %forecast.1.f_ref = bf16[4,4,2,64,5760]{4,3,2,1,0:T(8,128)(2,1)} custom-call(bf16[4,8,64,1440]{3,2,1,0:T(8,128)(2,1)} %x_ref.1, bf16[192,192]{1,0:T(8,128)(2,1)} %reshape.15.w_ref, f32[64,1]{1,0:T(8,128)} %copy.11.b_ref), custom_call_target="tpu_custom_call" | custom-call | tf_op jit(solution)/shard_map/forecast/pallas_call | solution.py:223
  152.6 15.0 %pick.1.p_ref = f32[8,2048]{1,0:T(8,128)} custom-call(s32[2048]{0:T(1024)} %fusion.5.index_ref, s32[2048,1]{1,0:T(8,128)} %copy.12.lane_ref, bf16[4,4,2,64,5760]{4,3,2,1,0:T(8,128)(2,1)} %forecast.1.f_ref), custom_call_target="tpu_custom_call" | custom-call | tf_op jit(solution)/shard_map/pick/pallas_call | solution.py:292
  167.6 61.5 %stats.1.k_ref = bf16[64,256]{1,0:T(8,128)(2,1)} custom-call(f32[8,2048]{1,0:T(8,128)} %pick.1.p_ref, f32[1,2048]{1,0:T(1,128)} %compare_convert_fusion.live_ref, f32[1,2048]{1,0:T(1,128)} %bitcast.9, f32[1,2048]{1,0:T(1,128)} %bitcast.10), custom_call_target="tpu_custom_call" | custom-call | tf_op jit(solution)/shard_map/stats/pallas_call | solution.py:406
  229.1 13.4 %mix.1 = bf16[4,8,64,1440]{3,2,1,0:T(8,128)(2,1)} custom-call(bf16[64,256]{1,0:T(8,128)(2,1)} %stats.1.k_ref, bf16[4,4,2,64,5760]{4,3,2,1,0:T(8,128)(2,1)} %forecast.1.f_ref), custom_call_target="tpu_custom_call" | custom-call | tf_op jit(solution)/shard_map/mix/pallas_call | solution.py:435

commit v2 on v1

v2 whole, which is shorter than its diff:
```python
import functools

import jax
import jax.numpy as jnp
from jax import lax
from jax.experimental import pallas as pl
from jax.experimental.pallas import tpu as pltpu
from jax.sharding import PartitionSpec as P

NS_STEPS = 16
LON = 1440
WIDE = 1536
MAIN = 1408
PACK = 5760
F32 = jnp.float32
BF16 = jnp.bfloat16
ORDER = (1, 2, 3, 0)
YBASE = {1: 1, 2: 2, 3: 6}
ANY = pl.BlockSpec(memory_space=pl.ANY)
VM = pl.BlockSpec(memory_space=pltpu.VMEM)
SM = pl.BlockSpec(memory_space=pltpu.SMEM)


def remote(src, dst, send, recv, peer):
    return pltpu.make_async_remote_copy(
        src_ref=src, dst_ref=dst, send_sem=send, recv_sem=recv, device_id=peer
    )


def widen(x):
    last = jnp.concatenate(
        [x[:, MAIN:LON], x[:, 0:32], x[:, 0:32], x[:, MAIN:LON]], axis=1
    )
    return jnp.concatenate([x[:, :MAIN], last], axis=1)


def conv_rows(src, count, weights, bias, acc_near, acc_far, emit):
    def body(q, carry):
        row = src[q]
        taps = jnp.concatenate(
            [pltpu.roll(row, 1, 1), row, pltpu.roll(row, WIDE - 1, 1)], axis=0
        )
        part = jnp.dot(weights, taps, preferred_element_type=F32)
        total = acc_near[...] + part[128:192]
        acc_near[...] = acc_far[...] + part[64:128]
        acc_far[...] = part[0:64]

        @pl.when(q >= 2)
        def _():
            center = src[q - 1].astype(F32)
            emit(q - 2, (center + jnp.tanh(total + bias)).astype(BF16))

        return carry

    lax.fori_loop(0, count, body, 0)


def forecast_kernel(
    x_ref, kernel_ref, offset_ref, position_ref, slots_ref, reading_ref, precision_ref,
    f_ref, mats_ref,
    xin, wide, mid, acc_near, acc_far, rem, fields, weights_ref, flat, slab, code, code_mem, lanes,
    relay, own_pred, preds, sums,
    load_sem, halo_send, halo_recv, relay_send, relay_recv, start_send, start_recv,
    keep_sem, y_send, y_recv, c_send, c_recv, g_send, g_recv, code_sem,
    p_send, p_recv, z_send, z_recv, s_send, s_recv, h_send, h_recv,
):
    g = lax.axis_index("member")
    b = lax.axis_index("band")
    ypeer = {"member": g ^ 2}
    cpeer = {"member": g ^ 1}
    up = {"band": lax.rem(b + 1, 32)}
    down = {"band": lax.rem(b + 31, 32)}
    z = lax.rem(b, 4)
    xx = lax.rem(b // 4, 4)
    hi = b // 16
    members = [ypeer, cpeer, {"member": g ^ 3}]
    zs = [{"band": b - z + lax.rem(z + d, 4)} for d in (1, 2, 3)]
    xs = [{"band": hi * 16 + lax.rem(xx + d, 4) * 4 + z} for d in (1, 2, 3)]
    far = {"band": lax.rem(b + 16, 32), "member": g ^ 2}
    edge_low = b == 15
    edge_high = b == 16
    edge = jnp.logical_or(edge_low, edge_high)
    relay_up = jnp.logical_and(b >= 23, z == 3)
    relay_down = jnp.logical_and(b <= 8, z == 0)
    relaying = jnp.logical_or(relay_up, relay_down)
    across = {"band": jnp.where(edge_low, 16, 15), "member": g ^ 2}

    barrier = pltpu.get_barrier_semaphore()
    for peer in members + zs + xs + [far, up, down]:
        pl.semaphore_signal(barrier, inc=1, device_id=peer)

    @pl.when(edge)
    def _():
        pl.semaphore_signal(barrier, inc=1, device_id=across)
        for band in (0, 4, 8, 23, 27, 31):
            pl.semaphore_signal(barrier, inc=1, device_id={"band": band})

    @pl.when(relaying)
    def _():
        for band in (15, 16):
            pl.semaphore_signal(barrier, inc=1, device_id={"band": band})

    def load(m):
        return pltpu.make_async_copy(x_ref.at[m], xin.at[m, 2:10], load_sem.at[m])

    for m in ORDER:
        load(m).start()
    pl.semaphore_wait(barrier, 12 + jnp.where(edge, 7, 0) + jnp.where(relaying, 2, 0))

    def halo_up(slot, src, peer=up):
        return remote(src, xin.at[slot, 0:2], halo_send.at[slot, 0], halo_recv.at[slot, 0], peer)

    def halo_down(slot, src, peer=down):
        return remote(src, xin.at[slot, 10:12], halo_send.at[slot, 1], halo_recv.at[slot, 1], peer)

    def to_relay(slot, src, side, band):
        return remote(src, relay, halo_send.at[slot, side], relay_recv, {"band": band})

    def own_halo(n):
        m = ORDER[n]
        high = x_ref.at[m, 6:8]
        low = x_ref.at[m, 0:2]
        plain_up = jnp.logical_and(b < 31, jnp.logical_not(edge_low)) if n else b < 31
        plain_down = jnp.logical_and(b > 0, jnp.logical_not(edge_high)) if n else b > 0

        @pl.when(plain_up)
        def _():
            halo_up(m, high).start()

        @pl.when(plain_down)
        def _():
            halo_down(m, low).start()

        if n:
            @pl.when(edge_low)
            def _():
                to_relay(m, high, 0, 19 + 4 * n).start()

            @pl.when(edge_high)
            def _():
                to_relay(m, low, 1, 12 - 4 * n).start()

    def start_copy():
        return remote(x_ref.at[0], xin.at[4, 2:10], start_send, start_recv, ypeer)

    own_halo(0)
    start_copy().start()
    for n in (1, 2, 3):
        own_halo(n)

    @pl.when(edge_low)
    def _():
        halo_up(4, x_ref.at[0, 6:8], across).start()

    @pl.when(edge_high)
    def _():
        halo_down(4, x_ref.at[0, 0:2], across).start()

    pos = position_ref[...]
    q5 = jnp.right_shift(pos, 5)
    flat_row = jnp.right_shift(q5 * 46604, 21)
    lon = pos - flat_row * LON
    row = jnp.right_shift(flat_row, 6)
    part = jnp.right_shift(row, 2)
    j = row - part * 4
    lane = jnp.where(lon < MAIN, j * MAIN + lon, 4 * MAIN + 32 * j + lon - MAIN)
    block = jnp.right_shift(lane, 7)
    code[...] = block * 128 + part * 64 + flat_row - row * 64
    lanes[...] = lane - block * 128
    to_scalar = pltpu.make_async_copy(code, code_mem, code_sem)
    to_scalar.start()

    for tap in range(3):
        weights_ref[64 * tap : 64 * tap + 64] = jnp.concatenate(
            [kernel_ref[tap, 0], kernel_ref[tap, 1], kernel_ref[tap, 2]], axis=1
        )
    square = (64, 64)
    diagonal = lax.broadcasted_iota(jnp.int32, square, 0) == lax.broadcasted_iota(jnp.int32, square, 1)
    bias = jnp.sum(
        jnp.where(diagonal, jnp.broadcast_to(offset_ref[...], square), 0.0), axis=1, keepdims=True
    )
    to_scalar.wait()

    def relay_copy(n):
        m = ORDER[n]
        return (
            remote(relay, xin.at[m, 0:2], relay_send, halo_recv.at[m, 0], {"band": 16}),
            remote(relay, xin.at[m, 10:12], relay_send, halo_recv.at[m, 1], {"band": 15}),
        )

    @pl.when(relaying)
    def _():
        to_relay(0, x_ref.at[0, 0:2], 0, 0).wait_recv()

    for n in (1, 2, 3):
        @pl.when(b == 19 + 4 * n)
        def _():
            relay_copy(n)[0].start()

        @pl.when(b == 12 - 4 * n)
        def _():
            relay_copy(n)[1].start()

    def keep(slot, d, m):
        return pltpu.make_async_copy(fields.at[slot], f_ref.at[d, m], keep_sem.at[slot])

    def piece(p, count):
        if count == 1:
            return (slice(None),) * 3
        if count == 4:
            return (p // 2, pl.ds(lax.rem(p, 2) * 32, 32), slice(None))
        return (p // 4, pl.ds(lax.rem(p, 4) * 16, 16), slice(None))

    def y_copy(m, p, count):
        at = piece(p, count)
        k = YBASE[m] + p
        return remote(
            fields.at[(m,) + at], f_ref.at[(2, m) + at], y_send.at[k], y_recv.at[k], ypeer
        )

    def g_copy(m, p, count):
        at = piece(p, count)
        k = YBASE[m] + p
        return remote(
            f_ref.at[(2, m) + at], f_ref.at[(3, m) + at], g_send.at[k], g_recv.at[k], cpeer
        )

    def start_g():
        return remote(fields.at[4], f_ref.at[3, 0], g_send.at[0], g_recv.at[0], cpeer)

    def c_copy(m):
        return remote(fields.at[m], f_ref.at[1, m], c_send.at[m], c_recv.at[m], cpeer)

    pred_copies = [
        remote(own_pred, preds.at[g], p_send.at[d], p_recv.at[d], members[d]) for d in range(3)
    ]

    def iteration(i, carry):
        slot = jnp.where(i == 4, 4, lax.rem(i + 1, 4))

        @pl.when(i < 4)
        def _():
            load(slot).wait()

        @pl.when(b > 0)
        def _():
            halo_up(slot, x_ref.at[0, 6:8]).wait_recv()

        @pl.when(b < 31)
        def _():
            halo_down(slot, x_ref.at[0, 0:2]).wait_recv()

        @pl.when(b == 0)
        def _():
            xin[slot, 0:2] = jnp.zeros((2, 64, LON), BF16)

        @pl.when(b == 31)
        def _():
            xin[slot, 10:12] = jnp.zeros((2, 64, LON), BF16)

        def spread(r, c):
            wide[r] = widen(xin[slot, r])
            return c

        lax.fori_loop(0, 12, spread, 0)
        weights = weights_ref[...]

        def emit_mid(r, value):
            mid[r] = value

        conv_rows(wide, 12, weights, bias, acc_near, acc_far, emit_mid)

        @pl.when(b == 0)
        def _():
            mid[0] = jnp.zeros((64, WIDE), BF16)

        @pl.when(b == 31)
        def _():
            mid[9] = jnp.zeros((64, WIDE), BF16)

        def emit_field(r, value):
            half = r // 4
            offset = pl.multiple_of(lax.rem(r, 4) * MAIN, 128)
            fields[slot, half, :, pl.ds(offset, MAIN)] = value[:, :MAIN]
            rem[r] = value[:, MAIN:WIDE]

        conv_rows(mid, 10, weights, bias, acc_near, acc_far, emit_field)
        lane = lax.broadcasted_iota(jnp.int32, (64, 128), 1)
        for half in range(2):
            tail = rem[4 * half]
            for j in range(1, 4):
                tail = jnp.where(lane < 32 * j, tail, pltpu.roll(rem[4 * half + j], 32 * j, 1))
            fields[slot, half, :, 4 * MAIN : PACK] = tail

        @pl.when(i < 4)
        def _():
            keep(slot, 0, slot).start()
            c_copy(slot).start()

        @pl.when(i == 0)
        def _():
            y_copy(1, 0, 1).start()

        @pl.when(i == 1)
        def _():
            for p in range(3):
                y_copy(2, p, 4).start()

        @pl.when(i == 2)
        def _():
            start_copy().wait_recv()

            @pl.when(jnp.logical_and(b < 31, jnp.logical_not(edge_low)))
            def _():
                halo_up(4, xin.at[4, 8:10]).start()

            @pl.when(jnp.logical_and(b > 0, jnp.logical_not(edge_high)))
            def _():
                halo_down(4, xin.at[4, 2:4]).start()

        @pl.when(i < 4)
        def _():
            for half in range(2):
                widen_field(fields.at[slot, half], flat.at[slot], half)

        @pl.when(i == 3)
        def _():
            pick_loop(code_mem, lanes, own_pred, flat, slab)
            for c in pred_copies:
                c.start()
            y_copy(2, 3, 4).start()
            for p in range(8):
                y_copy(3, p, 8).start()
            y_copy(1, 0, 1).wait_recv()
            g_copy(1, 0, 1).start()

        @pl.when(i == 4)
        def _():
            keep(4, 2, 0).start()
            start_g().start()

        return carry

    lax.fori_loop(0, 5, iteration, 0)

    for c in pred_copies:
        c.wait()
    preds[g] = own_pred[...]
    predicted = jnp.concatenate([preds[d, 0:4] for d in range(4)], axis=0)

    def line(ref):
        return jnp.concatenate([ref[n : n + 1] for n in range(16)], axis=1)

    live = (lax.broadcasted_iota(jnp.int32, (1, 2048), 1) < slots_ref[0]).astype(F32)
    mean = jnp.sum(predicted, axis=0, keepdims=True) * (1.0 / 16.0)
    anomaly = predicted - mean
    weighted = anomaly * (line(precision_ref) * live)
    gram = exact(weighted, anomaly, (((1,), (1,)), ((), ())))
    drive = jnp.sum(weighted * (line(reading_ref) - mean), axis=1, keepdims=True)
    pair = jnp.concatenate([gram, drive, jnp.zeros((16, 111), F32)], axis=1)

    def reduce(stage, place, pair, peers, sends, recvs):
        sums[stage, place] = pair
        copies = [
            remote(sums.at[stage, place], sums.at[stage, place], sends.at[d], recvs.at[d], peer)
            for d, peer in enumerate(peers)
        ]
        for c in copies:
            c.start()
        for c in copies:
            c.wait()

    reduce(0, z, pair, zs, z_send, z_recv)
    pair = (sums[0, 0] + sums[0, 1]) + (sums[0, 2] + sums[0, 3])
    reduce(1, xx, pair, xs, s_send, s_recv)
    pair = (sums[1, 0] + sums[1, 1]) + (sums[1, 2] + sums[1, 3])
    reduce(2, hi, pair, [far], h_send, h_recv)
    pair = sums[2, 0] + sums[2, 1]
    mixing = transform(pair[:, 0:16], pair[:, 16:17]).astype(BF16)
    mats_ref[...] = expand(mixing, g)

    for m, count in ((2, 4), (3, 8)):
        def forward(p, carry):
            y_copy(m, p, count).wait_recv()
            g_copy(m, p, count).start()
            return carry

        lax.fori_loop(0, count, forward, 0)

    start_copy().wait_send()
    for slot in range(5):
        keep(slot, 0, 0).wait()

        @pl.when(b < 31)
        def _():
            halo_up(slot, x_ref.at[0, 6:8]).wait_send()

        @pl.when(b > 0)
        def _():
            halo_down(slot, x_ref.at[0, 0:2]).wait_send()

    @pl.when(relaying)
    def _():
        relay_copy(1)[0].wait_send()

    start_g().wait()
    for m, count in ((1, 1), (2, 4), (3, 8)):
        def finish(p, carry):
            y_copy(m, p, count).wait_send()
            g_copy(m, p, count).wait()
            return carry

        lax.fori_loop(0, count, finish, 0)
    for m in range(4):
        c_copy(m).wait()


def run_forecast(x, kernel, offset, position, slots, reading, precision):
    dma = pltpu.SemaphoreType.DMA
    return pl.pallas_call(
        forecast_kernel,
        out_shape=(
            jax.ShapeDtypeStruct((4, 4, 2, 64, PACK), BF16),
            jax.ShapeDtypeStruct((64, 256), BF16),
        ),
        in_specs=[ANY, VM, VM, VM, SM, VM, VM],
        out_specs=(ANY, VM),
        scratch_shapes=[
            pltpu.VMEM((5, 12, 64, LON), BF16),
            pltpu.VMEM((12, 64, WIDE), BF16),
            pltpu.VMEM((10, 64, WIDE), BF16),
            pltpu.VMEM((64, WIDE), F32),
            pltpu.VMEM((64, WIDE), F32),
            pltpu.VMEM((8, 64, 128), BF16),
            pltpu.VMEM((5, 2, 64, PACK), BF16),
            pltpu.VMEM((192, 192), BF16),
            pltpu.VMEM((4, PACK, 128), F32),
            pltpu.VMEM((4, 128, 128), F32),
            pltpu.VMEM((16, 128), jnp.int32),
            pltpu.SMEM((16, 128), jnp.int32),
            pltpu.VMEM((16, 128), jnp.int32),
            pltpu.VMEM((2, 64, LON), BF16),
            pltpu.VMEM((8, 2048), F32),
            pltpu.VMEM((4, 8, 2048), F32),
            pltpu.VMEM((3, 4, 16, 128), F32),
            dma((4,)), dma((5, 2)), dma((5, 2)), dma, dma, dma, dma,
            dma((5,)), dma((14,)), dma((14,)), dma((4,)), dma((4,)), dma((14,)), dma((14,)), dma,
            dma((3,)), dma((3,)), dma((3,)), dma((3,)), dma((3,)), dma((3,)), dma((1,)), dma((1,)),
        ],
        compiler_params=pltpu.CompilerParams(
            collective_id=1, has_side_effects=True, vmem_limit_bytes=58 << 20
        ),
        name="forecast",
    )(x, kernel, offset, position, slots, reading, precision)


def widen_field(src, dst, half):
    for block in range(45):
        start = block * 128
        dst[start + half * 64 : start + half * 64 + 64, :] = src[:, start : start + 128].astype(F32)


def pick_loop(code_mem, lanes, p_ref, flat, slab):
    square = (128, 128)
    down = lax.broadcasted_iota(jnp.int32, square, 0)
    diagonal = down == lax.broadcasted_iota(jnp.int32, square, 1)

    def group(n, carry):
        def fetch(t, c):
            for u in range(8):
                slot = t * 8 + u
                place = code_mem[n, slot]
                for m in range(4):
                    slab[m, pl.ds(slot, 1), :] = flat[m, pl.ds(place, 1), :]
            return c

        lax.fori_loop(0, 16, fetch, 0)
        hot = jnp.where(down == lanes[pl.ds(n, 1), :], 1.0, 0.0).astype(BF16)
        picked = []
        for m in range(4):
            table = jnp.dot(slab[m].astype(BF16), hot, preferred_element_type=F32)
            picked.append(jnp.sum(jnp.where(diagonal, table, 0.0), axis=0, keepdims=True))
        picked.append(jnp.zeros((4, 128), F32))
        p_ref[:, pl.ds(pl.multiple_of(n * 128, 128), 128)] = jnp.concatenate(picked, axis=0)
        return carry

    lax.fori_loop(0, 16, group, 0)


def exact(a, b, dims=(((1,), (0,)), ((), ()))):
    return lax.dot_general(
        a, b, dims, precision=lax.Precision.HIGHEST, preferred_element_type=F32
    )


def transform(gram, drive):
    n = 16
    eye = (
        lax.broadcasted_iota(jnp.int32, (n, n), 0) == lax.broadcasted_iota(jnp.int32, (n, n), 1)
    ).astype(F32)
    system = eye + gram / (n - 1.0)
    scale = jnp.sum(jnp.sum(system * eye, axis=1, keepdims=True), axis=0, keepdims=True)
    iterate = system / scale
    root = eye
    for _ in range(NS_STEPS):
        factor = 0.5 * (3.0 * eye - exact(root, iterate))
        iterate = exact(iterate, factor)
        root = exact(factor, root)
    spread = root / jnp.sqrt(scale)
    mean_weights = exact(exact(root, root), drive) / (scale * (n - 1.0))
    centering = eye - 1.0 / n
    return 1.0 / n + exact(centering, mean_weights + spread)


def expand(mixing, g):
    def iota(shape, dim):
        return lax.broadcasted_iota(jnp.int32, shape, dim)

    own = (iota((64, 16), 1) == 4 * g + iota((64, 16), 0) // 16).astype(BF16)
    column = iota((16, 256), 1)
    source = 4 * jnp.bitwise_xor(column // 64, g) + lax.rem(column // 16, 4)
    order = (iota((16, 256), 0) == source).astype(BF16)
    picked = lax.dot_general(
        own, mixing, (((1,), (1,)), ((), ())), preferred_element_type=F32
    ).astype(BF16)
    full = jnp.dot(picked, order, preferred_element_type=F32)
    same = lax.rem(iota((64, 256), 0), 16) == lax.rem(iota((64, 256), 1), 16)
    return jnp.where(same, full, 0.0).astype(BF16)


def mix_kernel(k_ref, f_ref, o_ref):
    mats = k_ref[...]

    def product(lo, width):
        block = f_ref[:, :, 0, :, lo : lo + width].reshape(256, width)
        return jnp.dot(mats, block, preferred_element_type=F32).astype(BF16).reshape(4, 16, width)

    tail = product(4 * MAIN, 128)
    for j in range(4):
        o_ref[:, j, :, 0:MAIN] = product(j * MAIN, MAIN)
        o_ref[:, j, :, MAIN:LON] = tail[:, :, 32 * j : 32 * j + 32]


def run_mix(mats, fields):
    return pl.pallas_call(
        mix_kernel,
        grid=(2, 4),
        out_shape=jax.ShapeDtypeStruct((4, 8, 64, LON), BF16),
        in_specs=[
            pl.BlockSpec((64, 256), lambda h, c: (0, 0)),
            pl.BlockSpec((4, 4, 1, 16, PACK), lambda h, c: (0, 0, h, c, 0)),
        ],
        out_specs=pl.BlockSpec((4, 4, 16, LON), lambda h, c: (0, h, c, 0)),
        compiler_params=pltpu.CompilerParams(vmem_limit_bytes=56 << 20),
        name="mix",
    )(mats, fields)


def local(x, kernel, offset, position, slots, reading, precision):
    fields, mats = run_forecast(
        x,
        kernel,
        offset.reshape(1, 64),
        position.reshape(16, 128),
        slots,
        reading.reshape(16, 128),
        precision.reshape(16, 128),
    )
    return run_mix(mats, fields)


def solution(mesh):
    return jax.shard_map(
        local,
        mesh=mesh,
        in_specs=(
            P("member", "band", None, None), P(), P(), P("band"), P("band"), P("band"), P("band"),
        ),
        out_specs=P("member", "band", None, None),
        check_vma=False,
    )
```

time: 244 us -> 182 us (0.75)
  Pallas kernels: 235 us -> 181 us
  local copies, waits for them, and re-layouts: 4.54 us -> 0 us
  other arithmetic: 2.66 us -> 0 us
    pallas_call x3 -> x1, Pallas kernels: 221 us -> 168 us  [run_forecast(): pl.pallas_call(forecast_kernel, out_shape=(jax.ShapeDtypeStruct((4, 4, 2,...]
    broadcast_in_dim x2 -> x0, local copies, waits for them, and re-layouts: 2.69 us -> none  [the longest x1 1.35 us: local(): fields = run_forecast(x, weights, offset[:, None])]
where the time goes in v2:
time: 182 us
  Pallas kernels  181 us (99%)
    pallas_call x1, Pallas kernels, run_forecast(): pl.pallas_call(forecast_kernel, out_shape=(jax.ShapeDtypeStruct((4, 4, 2,...  168 us
    pallas_call x1, Pallas kernels, run_mix(): pl.pallas_call(mix_kernel, grid=(2, 4), out_shape=jax.ShapeDtypeStruct((4...  13.4 us

profile of v2, /device:TPU:1, one launch (start us, length us, event | category | flops | bytes accessed | tf_op | source)
XLA Modules:
  0.0 181.8 jit_solution(15763770377819231657)
XLA Ops:
  0.7 167.7 %forecast.1 = (bf16[4,4,2,64,5760]{4,3,2,1,0:T(8,128)(2,1)}, bf16[64,256]{1,0:T(8,128)(2,1)}) custom-call(bf16[4,8,64,1440]{3,2,1,0:T(8,128)(2,1)} %x_ref.1, bf16[3,3,64,64]{3,2,1,0:T(8,128)(2,1)} %kernel_ref.1, f32[1,64]{1,0:T(1,128)} %bitcast.7, s32[16,128]{1,0:T(8,128)} %bitcast.4, s32[1]{0:T(128)S(6)} %copy.8.slots_ref, f32[16,128]{1,0:T(8,128)} %bitcast.5, ...), custom_call_target="tpu_custom_call" | custom-call | tf_op jit(solution)/shard_map/forecast/pallas_call | solution.py:420
  168.4 13.4 %mix.1 = bf16[4,8,64,1440]{3,2,1,0:T(8,128)(2,1)} custom-call(bf16[64,256]{1,0:T(8,128)(2,1)} %get-tuple-element.7.k_ref, bf16[4,4,2,64,5760]{4,3,2,1,0:T(8,128)(2,1)} %get-tuple-element.8.f_ref), custom_call_target="tpu_custom_call" | custom-call | tf_op jit(solution)/shard_map/mix/pallas_call | solution.py:545

commit v3 on v2

--- a/solution.py
+++ b/solution.py
@@ -16,6 +16,10 @@
 BF16 = jnp.bfloat16
 ORDER = (1, 2, 3, 0)
 YBASE = {1: 1, 2: 2, 3: 6}
+RELAYS = (
+    (23, 0, 1), (27, 0, 2), (21, 0, 3), (22, 0, 4), (31, 0, 5),
+    (8, 1, 1), (4, 1, 2), (10, 1, 3), (9, 1, 4), (0, 1, 5),
+)
 ANY = pl.BlockSpec(memory_space=pl.ANY)
 VM = pl.BlockSpec(memory_space=pltpu.VMEM)
 SM = pl.BlockSpec(memory_space=pltpu.SMEM)
@@ -57,11 +61,11 @@
 
 def forecast_kernel(
     x_ref, kernel_ref, offset_ref, position_ref, slots_ref, reading_ref, precision_ref,
-    f_ref, mats_ref,
+    part_ref, last_ref, mats_ref,
     xin, wide, mid, acc_near, acc_far, rem, fields, weights_ref, flat, slab, code, code_mem, lanes,
-    relay, own_pred, preds, sums,
+    relay, own_pred, preds, sums, staged,
     load_sem, halo_send, halo_recv, relay_send, relay_recv, start_send, start_recv,
-    keep_sem, y_send, y_recv, c_send, c_recv, g_send, g_recv, code_sem,
+    last_sem, store_sem, y_send, y_recv, c_send, c_recv, g_send, g_recv, code_sem,
     p_send, p_recv, z_send, z_recv, s_send, s_recv, h_send, h_recv,
 ):
     g = lax.axis_index("member")
@@ -80,9 +84,7 @@
     edge_low = b == 15
     edge_high = b == 16
     edge = jnp.logical_or(edge_low, edge_high)
-    relay_up = jnp.logical_and(b >= 23, z == 3)
-    relay_down = jnp.logical_and(b <= 8, z == 0)
-    relaying = jnp.logical_or(relay_up, relay_down)
+    relaying = functools.reduce(jnp.logical_or, [b == band for band, _, _ in RELAYS])
     across = {"band": jnp.where(edge_low, 16, 15), "member": g ^ 2}
 
     barrier = pltpu.get_barrier_semaphore()
@@ -92,20 +94,25 @@
     @pl.when(edge)
     def _():
         pl.semaphore_signal(barrier, inc=1, device_id=across)
-        for band in (0, 4, 8, 23, 27, 31):
-            pl.semaphore_signal(barrier, inc=1, device_id={"band": band})
-
-    @pl.when(relaying)
-    def _():
-        for band in (15, 16):
-            pl.semaphore_signal(barrier, inc=1, device_id={"band": band})
+        for band, _, k in RELAYS:
+            pl.semaphore_signal(
+                barrier, inc=1, device_id={"band": band, "member": g ^ 2 if k > 2 else g}
+            )
+
+    for band, _, k in RELAYS:
+        @pl.when(b == band)
+        def _():
+            for target in (15, 16):
+                pl.semaphore_signal(
+                    barrier, inc=1, device_id={"band": target, "member": g ^ 2 if k > 2 else g}
+                )
 
     def load(m):
         return pltpu.make_async_copy(x_ref.at[m], xin.at[m, 2:10], load_sem.at[m])
 
     for m in ORDER:
         load(m).start()
-    pl.semaphore_wait(barrier, 12 + jnp.where(edge, 7, 0) + jnp.where(relaying, 2, 0))
+    pl.semaphore_wait(barrier, 12 + jnp.where(edge, 11, 0) + jnp.where(relaying, 2, 0))
 
     def halo_up(slot, src, peer=up):
         return remote(src, xin.at[slot, 0:2], halo_send.at[slot, 0], halo_recv.at[slot, 0], peer)
@@ -113,32 +120,45 @@
     def halo_down(slot, src, peer=down):
         return remote(src, xin.at[slot, 10:12], halo_send.at[slot, 1], halo_recv.at[slot, 1], peer)
 
-    def to_relay(slot, src, side, band):
-        return remote(src, relay, halo_send.at[slot, side], relay_recv, {"band": band})
+    def to_relay(slot, src, side, k):
+        band = next(band for band, s, n in RELAYS if (s, n) == (side, k))
+        peer = {"band": band, "member": g ^ 2 if k > 2 else g}
+        return remote(src, relay, halo_send.at[slot, side], relay_recv, peer)
+
+    def edge_rows(n):
+        m = ORDER[n]
+        for r in range(2):
+            k = 2 * n + r
+            for side, is_edge, source, row, peer in (
+                (0, edge_low, 6 + r, r, up), (1, edge_high, r, 10 + r, down),
+            ):
+                @pl.when(is_edge)
+                def _():
+                    src = x_ref.at[m, source : source + 1]
+                    if k:
+                        to_relay(m, src, side, k).start()
+                    else:
+                        remote(
+                            src, xin.at[m, row : row + 1],
+                            halo_send.at[m, side], halo_recv.at[m, side], peer,
+                        ).start()
+
+    not_low = jnp.logical_and(b < 31, jnp.logical_not(edge_low))
+    not_high = jnp.logical_and(b > 0, jnp.logical_not(edge_high))
 
     def own_halo(n):
         m = ORDER[n]
-        high = x_ref.at[m, 6:8]
-        low = x_ref.at[m, 0:2]
-        plain_up = jnp.logical_and(b < 31, jnp.logical_not(edge_low)) if n else b < 31
-        plain_down = jnp.logical_and(b > 0, jnp.logical_not(edge_high)) if n else b > 0
-
-        @pl.when(plain_up)
-        def _():
-            halo_up(m, high).start()
-
-        @pl.when(plain_down)
-        def _():
-            halo_down(m, low).start()
-
-        if n:
-            @pl.when(edge_low)
-            def _():
-                to_relay(m, high, 0, 19 + 4 * n).start()
-
-            @pl.when(edge_high)
-            def _():
-                to_relay(m, low, 1, 12 - 4 * n).start()
+
+        @pl.when(not_low)
+        def _():
+            halo_up(m, x_ref.at[m, 6:8]).start()
+
+        @pl.when(not_high)
+        def _():
+            halo_down(m, x_ref.at[m, 0:2]).start()
+
+        if n < 3:
+            edge_rows(n)
 
     def start_copy():
         return remote(x_ref.at[0], xin.at[4, 2:10], start_send, start_recv, ypeer)
@@ -181,28 +201,21 @@
     )
     to_scalar.wait()
 
-    def relay_copy(n):
-        m = ORDER[n]
-        return (
-            remote(relay, xin.at[m, 0:2], relay_send, halo_recv.at[m, 0], {"band": 16}),
-            remote(relay, xin.at[m, 10:12], relay_send, halo_recv.at[m, 1], {"band": 15}),
-        )
-
-    @pl.when(relaying)
-    def _():
-        to_relay(0, x_ref.at[0, 0:2], 0, 0).wait_recv()
-
-    for n in (1, 2, 3):
-        @pl.when(b == 19 + 4 * n)
-        def _():
-            relay_copy(n)[0].start()
-
-        @pl.when(b == 12 - 4 * n)
-        def _():
-            relay_copy(n)[1].start()
-
-    def keep(slot, d, m):
-        return pltpu.make_async_copy(fields.at[slot], f_ref.at[d, m], keep_sem.at[slot])
+    def relay_copy(side, k):
+        m = ORDER[k // 2]
+        row = (0 if side == 0 else 10) + k % 2
+        peer = {"band": 16 if side == 0 else 15, "member": g ^ 2 if k > 2 else g}
+        return remote(relay, xin.at[m, row : row + 1], relay_send, halo_recv.at[m, side], peer)
+
+    def relay_now(ks):
+        for band, side, k in RELAYS:
+            if k in ks:
+                @pl.when(b == band)
+                def _():
+                    remote(x_ref.at[0, 0:1], relay, relay_send, relay_recv, up).wait_recv()
+                    relay_copy(side, k).start()
+
+    relay_now((1,))
 
     def piece(p, count):
         if count == 1:
@@ -215,21 +228,21 @@
         at = piece(p, count)
         k = YBASE[m] + p
         return remote(
-            fields.at[(m,) + at], f_ref.at[(2, m) + at], y_send.at[k], y_recv.at[k], ypeer
+            fields.at[(0, m) + at], fields.at[(2, m) + at], y_send.at[k], y_recv.at[k], ypeer
         )
 
     def g_copy(m, p, count):
         at = piece(p, count)
         k = YBASE[m] + p
         return remote(
-            f_ref.at[(2, m) + at], f_ref.at[(3, m) + at], g_send.at[k], g_recv.at[k], cpeer
+            fields.at[(2, m) + at], fields.at[(3, m) + at], g_send.at[k], g_recv.at[k], cpeer
         )
 
     def start_g():
-        return remote(fields.at[4], f_ref.at[3, 0], g_send.at[0], g_recv.at[0], cpeer)
+        return remote(fields.at[2, 0], fields.at[3, 0], g_send.at[0], g_recv.at[0], cpeer)
 
     def c_copy(m):
-        return remote(fields.at[m], f_ref.at[1, m], c_send.at[m], c_recv.at[m], cpeer)
+        return remote(fields.at[0, m], fields.at[1, m], c_send.at[m], c_recv.at[m], cpeer)
 
     pred_copies = [
         remote(own_pred, preds.at[g], p_send.at[d], p_recv.at[d], members[d]) for d in range(3)
@@ -237,6 +250,8 @@
 
     def iteration(i, carry):
         slot = jnp.where(i == 4, 4, lax.rem(i + 1, 4))
+        home = jnp.where(i == 4, 2, 0)
+        own = lax.rem(slot, 4)
 
         @pl.when(i < 4)
         def _():
@@ -281,7 +296,7 @@
         def emit_field(r, value):
             half = r // 4
             offset = pl.multiple_of(lax.rem(r, 4) * MAIN, 128)
-            fields[slot, half, :, pl.ds(offset, MAIN)] = value[:, :MAIN]
+            fields[home, own, half, :, pl.ds(offset, MAIN)] = value[:, :MAIN]
             rem[r] = value[:, MAIN:WIDE]
 
         conv_rows(mid, 10, weights, bias, acc_near, acc_far, emit_field)
@@ -290,44 +305,52 @@
             tail = rem[4 * half]
             for j in range(1, 4):
                 tail = jnp.where(lane < 32 * j, tail, pltpu.roll(rem[4 * half + j], 32 * j, 1))
-            fields[slot, half, :, 4 * MAIN : PACK] = tail
+            fields[home, own, half, :, 4 * MAIN : PACK] = tail
 
         @pl.when(i < 4)
         def _():
-            keep(slot, 0, slot).start()
             c_copy(slot).start()
 
         @pl.when(i == 0)
         def _():
             y_copy(1, 0, 1).start()
 
+            relay_now((2, 3))
+
         @pl.when(i == 1)
         def _():
-            for p in range(3):
+            for p in range(2):
                 y_copy(2, p, 4).start()
-
-        @pl.when(i == 2)
-        def _():
+            relay_now((4, 5))
             start_copy().wait_recv()
 
-            @pl.when(jnp.logical_and(b < 31, jnp.logical_not(edge_low)))
+            @pl.when(not_low)
             def _():
                 halo_up(4, xin.at[4, 8:10]).start()
 
-            @pl.when(jnp.logical_and(b > 0, jnp.logical_not(edge_high)))
+            @pl.when(not_high)
             def _():
                 halo_down(4, xin.at[4, 2:4]).start()
 
+            @pl.when(edge_low)
+            def _():
+                halo_up(0, xin.at[4, 8:10], across).start()
+
+            @pl.when(edge_high)
+            def _():
+                halo_down(0, xin.at[4, 2:4], across).start()
+
         @pl.when(i < 4)
         def _():
             for half in range(2):
-                widen_field(fields.at[slot, half], flat.at[slot], half)
+                widen_field(fields.at[0, slot, half], flat.at[slot], half)
 
         @pl.when(i == 3)
         def _():
             pick_loop(code_mem, lanes, own_pred, flat, slab)
             for c in pred_copies:
                 c.start()
+            y_copy(2, 2, 4).start()
             y_copy(2, 3, 4).start()
             for p in range(8):
                 y_copy(3, p, 8).start()
@@ -336,7 +359,6 @@
 
         @pl.when(i == 4)
         def _():
-            keep(4, 2, 0).start()
             start_g().start()
 
         return carry
@@ -379,18 +401,87 @@
     mixing = transform(pair[:, 0:16], pair[:, 16:17]).astype(BF16)
     mats_ref[...] = expand(mixing, g)
 
-    for m, count in ((2, 4), (3, 8)):
-        def forward(p, carry):
+    mats = mats_ref[...]
+
+    def store(p):
+        out = part_ref.at[:, pl.ds(p // 4 * 4, 4), pl.ds(lax.rem(p, 4) * 16, 16), :]
+        return pltpu.make_async_copy(
+            staged.at[lax.rem(p, 2)], out, store_sem.at[lax.rem(p, 2)]
+        )
+
+    def mix(p):
+        half = p // 4
+        rows = pl.ds(pl.multiple_of(lax.rem(p, 4) * 16, 16), 16)
+
+        def product(lo, width):
+            block = fields[:, :, half, rows, lo : lo + width].reshape(256, width)
+            out = jnp.dot(mats, block, preferred_element_type=F32)
+            return out.astype(BF16).reshape(4, 16, width)
+
+        side = lax.rem(p, 2)
+        tail = product(4 * MAIN, 128)
+        for j in range(4):
+            staged[side, :, j, :, 0:MAIN] = product(j * MAIN, MAIN)
+            staged[side, :, j, :, MAIN:LON] = tail[:, :, 32 * j : 32 * j + 32]
+        store(p).start()
+
+    def forward(m, count):
+        def body(p, carry):
             y_copy(m, p, count).wait_recv()
             g_copy(m, p, count).start()
             return carry
 
-        lax.fori_loop(0, count, forward, 0)
+        lax.fori_loop(0, count, body, 0)
+
+    forward(2, 4)
+    g_copy(1, 0, 1).wait_recv()
+    start_g().wait_recv()
+    for m in range(4):
+        c_copy(m).wait_recv()
+
+    def last_copy(d, m):
+        return pltpu.make_async_copy(
+            fields.at[d, m, 1, 48:64], last_ref.at[d, m], last_sem.at[4 * d + m]
+        )
+
+    def early(p, carry):
+        g_copy(2, p, 4).wait_recv()
+        return carry
+
+    lax.fori_loop(0, 4, early, 0)
+    for d in range(4):
+        for m in range(4):
+            if d < 2 or m < 3:
+                last_copy(d, m).start()
+
+    def blend(p, carry):
+        y_copy(3, p, 8).wait_recv()
+        g_copy(3, p, 8).start()
+
+        @pl.when(p > 0)
+        def _():
+            g_copy(3, p - 1, 8).wait_recv()
+
+            @pl.when(p > 2)
+            def _():
+                store(p - 3).wait()
+
+            mix(p - 1)
+
+        return carry
+
+    lax.fori_loop(0, 8, blend, 0)
+    last_copy(2, 3).start()
+    g_copy(3, 7, 8).wait_recv()
+    last_copy(3, 3).start()
+    store(5).wait()
+    store(6).wait()
+    for d in range(4):
+        for m in range(4):
+            last_copy(d, m).wait()
 
     start_copy().wait_send()
     for slot in range(5):
-        keep(slot, 0, 0).wait()
-
         @pl.when(b < 31)
         def _():
             halo_up(slot, x_ref.at[0, 6:8]).wait_send()
@@ -401,18 +492,18 @@
 
     @pl.when(relaying)
     def _():
-        relay_copy(1)[0].wait_send()
-
-    start_g().wait()
+        relay_copy(0, 1).wait_send()
+
+    start_g().wait_send()
     for m, count in ((1, 1), (2, 4), (3, 8)):
         def finish(p, carry):
             y_copy(m, p, count).wait_send()
-            g_copy(m, p, count).wait()
+            g_copy(m, p, count).wait_send()
             return carry
 
         lax.fori_loop(0, count, finish, 0)
     for m in range(4):
-        c_copy(m).wait()
+        c_copy(m).wait_send()
 
 
 def run_forecast(x, kernel, offset, position, slots, reading, precision):
@@ -420,11 +511,12 @@
     return pl.pallas_call(
         forecast_kernel,
         out_shape=(
-            jax.ShapeDtypeStruct((4, 4, 2, 64, PACK), BF16),
+            jax.ShapeDtypeStruct((4, 8, 64, LON), BF16),
+            jax.ShapeDtypeStruct((4, 4, 16, PACK), BF16),
             jax.ShapeDtypeStruct((64, 256), BF16),
         ),
         in_specs=[ANY, VM, VM, VM, SM, VM, VM],
-        out_specs=(ANY, VM),
+        out_specs=(ANY, ANY, VM),
         scratch_shapes=[
             pltpu.VMEM((5, 12, 64, LON), BF16),
             pltpu.VMEM((12, 64, WIDE), BF16),
@@ -432,19 +524,20 @@
             pltpu.VMEM((64, WIDE), F32),
             pltpu.VMEM((64, WIDE), F32),
             pltpu.VMEM((8, 64, 128), BF16),
-            pltpu.VMEM((5, 2, 64, PACK), BF16),
+            pltpu.VMEM((4, 4, 2, 64, PACK), BF16),
             pltpu.VMEM((192, 192), BF16),
             pltpu.VMEM((4, PACK, 128), F32),
             pltpu.VMEM((4, 128, 128), F32),
             pltpu.VMEM((16, 128), jnp.int32),
             pltpu.SMEM((16, 128), jnp.int32),
             pltpu.VMEM((16, 128), jnp.int32),
-            pltpu.VMEM((2, 64, LON), BF16),
+            pltpu.VMEM((1, 64, LON), BF16),
             pltpu.VMEM((8, 2048), F32),
             pltpu.VMEM((4, 8, 2048), F32),
             pltpu.VMEM((3, 4, 16, 128), F32),
+            pltpu.VMEM((2, 4, 4, 16, LON), BF16),
             dma((4,)), dma((5, 2)), dma((5, 2)), dma, dma, dma, dma,
-            dma((5,)), dma((14,)), dma((14,)), dma((4,)), dma((4,)), dma((14,)), dma((14,)), dma,
+            dma((16,)), dma((2,)), dma((14,)), dma((14,)), dma((4,)), dma((4,)), dma((14,)), dma((14,)), dma,
             dma((3,)), dma((3,)), dma((3,)), dma((3,)), dma((3,)), dma((3,)), dma((1,)), dma((1,)),
         ],
         compiler_params=pltpu.CompilerParams(
@@ -528,36 +621,47 @@
     return jnp.where(same, full, 0.0).astype(BF16)
 
 
-def mix_kernel(k_ref, f_ref, o_ref):
+def finish_kernel(k_ref, last_ref, part_ref, o_ref):
+    step = pl.program_id(0)
     mats = k_ref[...]
 
-    def product(lo, width):
-        block = f_ref[:, :, 0, :, lo : lo + width].reshape(256, width)
-        return jnp.dot(mats, block, preferred_element_type=F32).astype(BF16).reshape(4, 16, width)
-
-    tail = product(4 * MAIN, 128)
-    for j in range(4):
-        o_ref[:, j, :, 0:MAIN] = product(j * MAIN, MAIN)
-        o_ref[:, j, :, MAIN:LON] = tail[:, :, 32 * j : 32 * j + 32]
-
-
-def run_mix(mats, fields):
+    @pl.when(step < 3)
+    def _():
+        o_ref[...] = part_ref[...]
+
+    @pl.when(step == 3)
+    def _():
+        o_ref[:, :, 0:16] = part_ref[:, :, 0:16]
+
+        def product(lo, width):
+            block = last_ref[:, :, :, lo : lo + width].reshape(256, width)
+            out = jnp.dot(mats, block, preferred_element_type=F32)
+            return out.astype(BF16).reshape(4, 16, width)
+
+        tail = product(4 * MAIN, 128)
+        for j in range(4):
+            o_ref[:, j, 16:32, 0:MAIN] = product(j * MAIN, MAIN)
+            o_ref[:, j, 16:32, MAIN:LON] = tail[:, :, 32 * j : 32 * j + 32]
+
+
+def run_finish(mats, last, part):
     return pl.pallas_call(
-        mix_kernel,
-        grid=(2, 4),
+        finish_kernel,
+        grid=(4,),
         out_shape=jax.ShapeDtypeStruct((4, 8, 64, LON), BF16),
         in_specs=[
-            pl.BlockSpec((64, 256), lambda h, c: (0, 0)),
-            pl.BlockSpec((4, 4, 1, 16, PACK), lambda h, c: (0, 0, h, c, 0)),
+            pl.BlockSpec((64, 256), lambda i: (0, 0)),
+            pl.BlockSpec((4, 4, 16, PACK), lambda i: (0, 0, 0, 0)),
+            pl.BlockSpec((4, 4, 32, LON), lambda i: (0, i // 2, i % 2, 0)),
         ],
-        out_specs=pl.BlockSpec((4, 4, 16, LON), lambda h, c: (0, h, c, 0)),
-        compiler_params=pltpu.CompilerParams(vmem_limit_bytes=56 << 20),
-        name="mix",
-    )(mats, fields)
+        out_specs=pl.BlockSpec((4, 4, 32, LON), lambda i: (0, i // 2, i % 2, 0)),
+        compiler_params=pltpu.CompilerParams(vmem_limit_bytes=60 << 20),
+        name="finish",
+    )(mats, last, part)
 
 
 def local(x, kernel, offset, position, slots, reading, precision):
-    fields, mats = run_forecast(
+    part, last, mats = run_forecast(
         x,
         kernel,
         offset.reshape(1, 64),
@@ -566,7 +670,7 @@
         reading.reshape(16, 128),
         precision.reshape(16, 128),
     )
-    return run_mix(mats, fields)
+    return run_finish(mats, last, part)
 
 
 def solution(mesh):

time: 182 us -> 156 us (0.86)
  Pallas kernels: 181 us -> 155 us
    pallas_call x2, Pallas kernels: 181 us -> 155 us  [the longest x1 147 us: run_forecast(): pl.pallas_call(forecast_kernel, out_shape=(jax.ShapeDtypeStruct((4, 8, 64...]
where the time goes in v3:
time: 156 us; the launch traced here: 155 us
  Pallas kernels  155 us (99%)
    pallas_call x1, Pallas kernels, run_forecast(): pl.pallas_call(forecast_kernel, out_shape=(jax.ShapeDtypeStruct((4, 8, 64...  147 us
    pallas_call x1, Pallas kernels, run_finish(): pl.pallas_call(finish_kernel, grid=(4,), out_shape=jax.ShapeDtypeStruct((...  7.29 us

profile of v3, /device:TPU:1, one launch (start us, length us, event | category | flops | bytes accessed | tf_op | source)
XLA Modules:
  0.0 155.4 jit_solution(16442095053111428995)
XLA Ops:
  0.7 147.5 %forecast.1 = (bf16[4,8,64,1440]{3,2,1,0:T(8,128)(2,1)}, bf16[4,4,16,5760]{3,2,1,0:T(8,128)(2,1)}, bf16[64,256]{1,0:T(8,128)(2,1)}) custom-call(bf16[4,8,64,1440]{3,2,1,0:T(8,128)(2,1)} %x_ref.1, bf16[3,3,64,64]{3,2,1,0:T(8,128)(2,1)} %kernel_ref.1, f32[1,64]{1,0:T(1,128)} %bitcast.7, s32[16,128]{1,0:T(8,128)} %bitcast.4, s32[1]{0:T(128)S(6)} %copy.8.slots_ref, ...), custom_call_target="tpu_custom_call" | custom-call | tf_op jit(solution)/shard_map/forecast/pallas_call | solution.py:511
  148.1 7.3 %finish.1 = bf16[4,8,64,1440]{3,2,1,0:T(8,128)(2,1)} custom-call(bf16[64,256]{1,0:T(8,128)(2,1)} %get-tuple-element.8.k_ref, bf16[4,4,16,5760]{3,2,1,0:T(8,128)(2,1)} %get-tuple-element.9.last_ref, bf16[4,8,64,1440]{3,2,1,0:T(8,128)(2,1)} %get-tuple-element.10.part_ref), custom_call_target="tpu_custom_call" | custom-call | tf_op jit(solution)/shard_map/finish/pallas_call | solution.py:648

commit v4 on v3

--- a/solution.py
+++ b/solution.py
@@ -61,11 +61,11 @@
 
 def forecast_kernel(
     x_ref, kernel_ref, offset_ref, position_ref, slots_ref, reading_ref, precision_ref,
-    part_ref, last_ref, mats_ref,
-    xin, wide, mid, acc_near, acc_far, rem, fields, weights_ref, flat, slab, code, code_mem, lanes,
-    relay, own_pred, preds, sums, staged,
+    part_ref,
+    mats_ref, xin, wide, mid, acc_near, acc_far, rem, fields, weights_ref, flat, slab, code, code_mem, lanes,
+    relay, own_pred, preds, sums,
     load_sem, halo_send, halo_recv, relay_send, relay_recv, start_send, start_recv,
-    last_sem, store_sem, y_send, y_recv, c_send, c_recv, g_send, g_recv, code_sem,
+    y_send, y_recv, c_send, c_recv, g_send, g_recv, code_sem,
     p_send, p_recv, z_send, z_recv, s_send, s_recv, h_send, h_recv,
 ):
     g = lax.axis_index("member")
@@ -319,7 +319,7 @@
 
         @pl.when(i == 1)
         def _():
-            for p in range(2):
+            for p in range(3):
                 y_copy(2, p, 4).start()
             relay_now((4, 5))
             start_copy().wait_recv()
@@ -350,7 +350,6 @@
             pick_loop(code_mem, lanes, own_pred, flat, slab)
             for c in pred_copies:
                 c.start()
-            y_copy(2, 2, 4).start()
             y_copy(2, 3, 4).start()
             for p in range(8):
                 y_copy(3, p, 8).start()
@@ -403,12 +402,6 @@
 
     mats = mats_ref[...]
 
-    def store(p):
-        out = part_ref.at[:, pl.ds(p // 4 * 4, 4), pl.ds(lax.rem(p, 4) * 16, 16), :]
-        return pltpu.make_async_copy(
-            staged.at[lax.rem(p, 2)], out, store_sem.at[lax.rem(p, 2)]
-        )
-
     def mix(p):
         half = p // 4
         rows = pl.ds(pl.multiple_of(lax.rem(p, 4) * 16, 16), 16)
@@ -418,12 +411,10 @@
             out = jnp.dot(mats, block, preferred_element_type=F32)
             return out.astype(BF16).reshape(4, 16, width)
 
-        side = lax.rem(p, 2)
         tail = product(4 * MAIN, 128)
         for j in range(4):
-            staged[side, :, j, :, 0:MAIN] = product(j * MAIN, MAIN)
-            staged[side, :, j, :, MAIN:LON] = tail[:, :, 32 * j : 32 * j + 32]
-        store(p).start()
+            part_ref[:, 4 * half + j, rows, 0:MAIN] = product(j * MAIN, MAIN)
+            part_ref[:, 4 * half + j, rows, MAIN:LON] = tail[:, :, 32 * j : 32 * j + 32]
 
     def forward(m, count):
         def body(p, carry):
@@ -439,21 +430,11 @@
     for m in range(4):
         c_copy(m).wait_recv()
 
-    def last_copy(d, m):
-        return pltpu.make_async_copy(
-            fields.at[d, m, 1, 48:64], last_ref.at[d, m], last_sem.at[4 * d + m]
-        )
-
     def early(p, carry):
         g_copy(2, p, 4).wait_recv()
         return carry
 
     lax.fori_loop(0, 4, early, 0)
-    for d in range(4):
-        for m in range(4):
-            if d < 2 or m < 3:
-                last_copy(d, m).start()
-
     def blend(p, carry):
         y_copy(3, p, 8).wait_recv()
         g_copy(3, p, 8).start()
@@ -461,25 +442,13 @@
         @pl.when(p > 0)
         def _():
             g_copy(3, p - 1, 8).wait_recv()
-
-            @pl.when(p > 2)
-            def _():
-                store(p - 3).wait()
-
             mix(p - 1)
 
         return carry
 
     lax.fori_loop(0, 8, blend, 0)
-    last_copy(2, 3).start()
     g_copy(3, 7, 8).wait_recv()
-    last_copy(3, 3).start()
-    store(5).wait()
-    store(6).wait()
-    for d in range(4):
-        for m in range(4):
-            last_copy(d, m).wait()
-
+    mix(7)
     start_copy().wait_send()
     for slot in range(5):
         @pl.when(b < 31)
@@ -510,14 +479,11 @@
     dma = pltpu.SemaphoreType.DMA
     return pl.pallas_call(
         forecast_kernel,
-        out_shape=(
-            jax.ShapeDtypeStruct((4, 8, 64, LON), BF16),
-            jax.ShapeDtypeStruct((4, 4, 16, PACK), BF16),
-            jax.ShapeDtypeStruct((64, 256), BF16),
-        ),
+        out_shape=pltpu.VMEM((4, 8, 64, LON), BF16),
         in_specs=[ANY, VM, VM, VM, SM, VM, VM],
-        out_specs=(ANY, ANY, VM),
+        out_specs=VM,
         scratch_shapes=[
+            pltpu.VMEM((64, 256), BF16),
             pltpu.VMEM((5, 12, 64, LON), BF16),
             pltpu.VMEM((12, 64, WIDE), BF16),
             pltpu.VMEM((10, 64, WIDE), BF16),
@@ -535,13 +501,12 @@
             pltpu.VMEM((8, 2048), F32),
             pltpu.VMEM((4, 8, 2048), F32),
             pltpu.VMEM((3, 4, 16, 128), F32),
-            pltpu.VMEM((2, 4, 4, 16, LON), BF16),
             dma((4,)), dma((5, 2)), dma((5, 2)), dma, dma, dma, dma,
-            dma((16,)), dma((2,)), dma((14,)), dma((14,)), dma((4,)), dma((4,)), dma((14,)), dma((14,)), dma,
+            dma((14,)), dma((14,)), dma((4,)), dma((4,)), dma((14,)), dma((14,)), dma,
             dma((3,)), dma((3,)), dma((3,)), dma((3,)), dma((3,)), dma((3,)), dma((1,)), dma((1,)),
         ],
         compiler_params=pltpu.CompilerParams(
-            collective_id=1, has_side_effects=True, vmem_limit_bytes=58 << 20
+            collective_id=1, has_side_effects=True, vmem_limit_bytes=53 << 20
         ),
         name="forecast",
     )(x, kernel, offset, position, slots, reading, precision)
@@ -621,47 +586,33 @@
     return jnp.where(same, full, 0.0).astype(BF16)
 
 
-def finish_kernel(k_ref, last_ref, part_ref, o_ref):
-    step = pl.program_id(0)
-    mats = k_ref[...]
-
-    @pl.when(step < 3)
-    def _():
-        o_ref[...] = part_ref[...]
-
-    @pl.when(step == 3)
-    def _():
-        o_ref[:, :, 0:16] = part_ref[:, :, 0:16]
-
-        def product(lo, width):
-            block = last_ref[:, :, :, lo : lo + width].reshape(256, width)
-            out = jnp.dot(mats, block, preferred_element_type=F32)
-            return out.astype(BF16).reshape(4, 16, width)
-
-        tail = product(4 * MAIN, 128)
-        for j in range(4):
-            o_ref[:, j, 16:32, 0:MAIN] = product(j * MAIN, MAIN)
-            o_ref[:, j, 16:32, MAIN:LON] = tail[:, :, 32 * j : 32 * j + 32]
-
-
-def run_finish(mats, last, part):
+def finish_kernel(part_ref, o_ref, sem):
+    copies = [
+        pltpu.make_async_copy(
+            part_ref.at[n // 2, pl.ds(n % 2 * 4, 4)], o_ref.at[n // 2, pl.ds(n % 2 * 4, 4)], sem.at[n]
+        )
+        for n in range(8)
+    ]
+    for copy in copies:
+        copy.start()
+    for copy in copies:
+        copy.wait()
+
+
+def run_finish(part):
     return pl.pallas_call(
         finish_kernel,
-        grid=(4,),
         out_shape=jax.ShapeDtypeStruct((4, 8, 64, LON), BF16),
-        in_specs=[
-            pl.BlockSpec((64, 256), lambda i: (0, 0)),
-            pl.BlockSpec((4, 4, 16, PACK), lambda i: (0, 0, 0, 0)),
-            pl.BlockSpec((4, 4, 32, LON), lambda i: (0, i // 2, i % 2, 0)),
-        ],
-        out_specs=pl.BlockSpec((4, 4, 32, LON), lambda i: (0, i // 2, i % 2, 0)),
-        compiler_params=pltpu.CompilerParams(vmem_limit_bytes=60 << 20),
+        in_specs=[VM],
+        out_specs=ANY,
+        scratch_shapes=[pltpu.SemaphoreType.DMA((8,))],
+        compiler_params=pltpu.CompilerParams(vmem_limit_bytes=1 << 20),
         name="finish",
-    )(mats, last, part)
+    )(part)
 
 
 def local(x, kernel, offset, position, slots, reading, precision):
-    part, last, mats = run_forecast(
+    part = run_forecast(
         x,
         kernel,
         offset.reshape(1, 64),
@@ -670,7 +621,7 @@
         reading.reshape(16, 128),
         precision.reshape(16, 128),
     )
-    return run_finish(mats, last, part)
+    return run_finish(part)
 
 
 def solution(mesh):

time: 156 us -> 150 us (0.962)
  Pallas kernels: 155 us -> 149 us
    pallas_call x2, Pallas kernels: 155 us -> 149 us  [the longest x1 147 us: run_forecast(): pl.pallas_call(forecast_kernel, out_shape=pltpu.VMEM((4, 8, 64, LON), BF1...]
where the time goes in v4:
time: 150 us
  Pallas kernels  149 us (99%)
    pallas_call x1, Pallas kernels, run_forecast(): pl.pallas_call(forecast_kernel, out_shape=pltpu.VMEM((4, 8, 64, LON), BF1...  147 us

profile of v4, /device:TPU:1, one launch (start us, length us, event | category | flops | bytes accessed | tf_op | source)
XLA Modules:
  0.0 150.0 jit_solution(7146402632468574959)
XLA Ops:
  0.7 146.6 %forecast.1.part_ref = bf16[4,8,64,1440]{3,2,1,0:T(8,128)(2,1)S(1)} custom-call(bf16[4,8,64,1440]{3,2,1,0:T(8,128)(2,1)} %x_ref.1, bf16[3,3,64,64]{3,2,1,0:T(8,128)(2,1)} %kernel_ref.1, f32[1,64]{1,0:T(1,128)} %bitcast.7, s32[16,128]{1,0:T(8,128)} %bitcast.4, s32[1]{0:T(128)S(6)} %copy.8.slots_ref, f32[16,128]{1,0:T(8,128)} %bitcast.5, f32[16,128]{1,0:T(8,128)} %bitcast.6), custom_call_target="tpu_custom_call" | custom-call | tf_op jit(solution)/shard_map/forecast/pallas_call | solution.py:480
  147.3 2.7 %finish.1 = bf16[4,8,64,1440]{3,2,1,0:T(8,128)(2,1)} custom-call(bf16[4,8,64,1440]{3,2,1,0:T(8,128)(2,1)S(1)} %forecast.1.part_ref), custom_call_target="tpu_custom_call" | custom-call | tf_op jit(solution)/shard_map/finish/pallas_call | solution.py:603

commit v5 on v4

--- a/solution.py
+++ b/solution.py
@@ -63,7 +63,7 @@
     x_ref, kernel_ref, offset_ref, position_ref, slots_ref, reading_ref, precision_ref,
     part_ref,
     mats_ref, xin, wide, mid, acc_near, acc_far, rem, fields, weights_ref, flat, slab, code, code_mem, lanes,
-    relay, own_pred, preds, sums,
+    relay, own_pred, dense, tail_out, tail_in, preds, sums,
     load_sem, halo_send, halo_recv, relay_send, relay_recv, start_send, start_recv,
     y_send, y_recv, c_send, c_recv, g_send, g_recv, code_sem,
     p_send, p_recv, z_send, z_recv, s_send, s_recv, h_send, h_recv,
@@ -110,7 +110,7 @@
     def load(m):
         return pltpu.make_async_copy(x_ref.at[m], xin.at[m, 2:10], load_sem.at[m])
 
-    for m in ORDER:
+    for m in (0, 1, 2, 3):
         load(m).start()
     pl.semaphore_wait(barrier, 12 + jnp.where(edge, 11, 0) + jnp.where(relaying, 2, 0))
 
@@ -161,7 +161,13 @@
             edge_rows(n)
 
     def start_copy():
-        return remote(x_ref.at[0], xin.at[4, 2:10], start_send, start_recv, ypeer)
+        return remote(
+            x_ref.at[0, :, :, 0:MAIN], xin.at[4, 2:10, :, 0:MAIN],
+            start_send.at[0], start_recv.at[0], ypeer,
+        )
+
+    def tail_copy():
+        return remote(tail_out, tail_in, start_send.at[1], start_recv.at[1], ypeer)
 
     own_halo(0)
     start_copy().start()
@@ -175,6 +181,13 @@
     @pl.when(edge_high)
     def _():
         halo_down(4, x_ref.at[0, 0:2], across).start()
+
+    load(0).wait()
+    for half in range(2):
+        tail_out[half] = jnp.concatenate(
+            [xin[0, 2 + 4 * half + j, :, MAIN:LON] for j in range(4)], axis=1
+        )
+    tail_copy().start()
 
     pos = position_ref[...]
     q5 = jnp.right_shift(pos, 5)
@@ -245,7 +258,7 @@
         return remote(fields.at[0, m], fields.at[1, m], c_send.at[m], c_recv.at[m], cpeer)
 
     pred_copies = [
-        remote(own_pred, preds.at[g], p_send.at[d], p_recv.at[d], members[d]) for d in range(3)
+        remote(dense, preds.at[g], p_send.at[d], p_recv.at[d], members[d]) for d in range(3)
     ]
 
     def iteration(i, carry):
@@ -253,7 +266,7 @@
         home = jnp.where(i == 4, 2, 0)
         own = lax.rem(slot, 4)
 
-        @pl.when(i < 4)
+        @pl.when(i < 3)
         def _():
             load(slot).wait()
 
@@ -323,6 +336,10 @@
                 y_copy(2, p, 4).start()
             relay_now((4, 5))
             start_copy().wait_recv()
+            tail_copy().wait_recv()
+            for half in range(2):
+                for j in range(4):
+                    xin[4, 2 + 4 * half + j, :, MAIN:LON] = tail_in[half, :, 32 * j : 32 * j + 32]
 
             @pl.when(not_low)
             def _():
@@ -348,6 +365,10 @@
         @pl.when(i == 3)
         def _():
             pick_loop(code_mem, lanes, own_pred, flat, slab)
+            dense[...] = jnp.concatenate(
+                [own_pred[m : m + 1, 512 * q : 512 * q + 512] for m in range(4) for q in range(4)],
+                axis=0,
+            ).astype(BF16)
             for c in pred_copies:
                 c.start()
             y_copy(2, 3, 4).start()
@@ -366,8 +387,16 @@
 
     for c in pred_copies:
         c.wait()
-    preds[g] = own_pred[...]
-    predicted = jnp.concatenate([preds[d, 0:4] for d in range(4)], axis=0)
+    preds[g] = dense[...]
+    quarters = preds[...].astype(F32)
+    predicted = jnp.concatenate(
+        [
+            jnp.concatenate([quarters[d, 4 * m + q : 4 * m + q + 1] for q in range(4)], axis=1)
+            for d in range(4)
+            for m in range(4)
+        ],
+        axis=0,
+    )
 
     def line(ref):
         return jnp.concatenate([ref[n : n + 1] for n in range(16)], axis=1)
@@ -450,6 +479,7 @@
     g_copy(3, 7, 8).wait_recv()
     mix(7)
     start_copy().wait_send()
+    tail_copy().wait_send()
     for slot in range(5):
         @pl.when(b < 31)
         def _():
@@ -499,9 +529,12 @@
             pltpu.VMEM((16, 128), jnp.int32),
             pltpu.VMEM((1, 64, LON), BF16),
             pltpu.VMEM((8, 2048), F32),
-            pltpu.VMEM((4, 8, 2048), F32),
+            pltpu.VMEM((16, 512), BF16),
+            pltpu.VMEM((2, 64, 128), BF16),
+            pltpu.VMEM((2, 64, 128), BF16),
+            pltpu.VMEM((4, 16, 512), BF16),
             pltpu.VMEM((3, 4, 16, 128), F32),
-            dma((4,)), dma((5, 2)), dma((5, 2)), dma, dma, dma, dma,
+            dma((4,)), dma((5, 2)), dma((5, 2)), dma, dma, dma((2,)), dma((2,)),
             dma((14,)), dma((14,)), dma((4,)), dma((4,)), dma((14,)), dma((14,)), dma,
             dma((3,)), dma((3,)), dma((3,)), dma((3,)), dma((3,)), dma((3,)), dma((1,)), dma((1,)),
         ],

time: 150 us -> 146 us (0.973)
  Pallas kernels: 149 us -> 145 us
    pallas_call x1, Pallas kernels: 147 us -> 142 us  [run_forecast(): pl.pallas_call(forecast_kernel, out_shape=pltpu.VMEM((4, 8, 64, LON), BF1...]
where the time goes in v5:
time: 146 us
  Pallas kernels  145 us (99%)
    pallas_call x1, Pallas kernels, run_forecast(): pl.pallas_call(forecast_kernel, out_shape=pltpu.VMEM((4, 8, 64, LON), BF1...  142 us

profile of v5, /device:TPU:1, one launch (start us, length us, event | category | flops | bytes accessed | tf_op | source)
XLA Modules:
  0.0 145.8 jit_solution(6533457799890821743)
XLA Ops:
  0.7 142.4 %forecast.1.part_ref = bf16[4,8,64,1440]{3,2,1,0:T(8,128)(2,1)S(1)} custom-call(bf16[4,8,64,1440]{3,2,1,0:T(8,128)(2,1)} %x_ref.1, bf16[3,3,64,64]{3,2,1,0:T(8,128)(2,1)} %kernel_ref.1, f32[1,64]{1,0:T(1,128)} %bitcast.7, s32[16,128]{1,0:T(8,128)} %bitcast.4, s32[1]{0:T(128)S(6)} %copy.8.slots_ref, f32[16,128]{1,0:T(8,128)} %bitcast.5, f32[16,128]{1,0:T(8,128)} %bitcast.6), custom_call_target="tpu_custom_call" | custom-call | tf_op jit(solution)/shard_map/forecast/pallas_call | solution.py:510
  143.1 2.7 %finish.1 = bf16[4,8,64,1440]{3,2,1,0:T(8,128)(2,1)} custom-call(bf16[4,8,64,1440]{3,2,1,0:T(8,128)(2,1)S(1)} %forecast.1.part_ref), custom_call_target="tpu_custom_call" | custom-call | tf_op jit(solution)/shard_map/finish/pallas_call | solution.py:636
